TPU v7x, 256 devices: a whole 4x4x8 slice. The times are simulated.
256 devices in a mesh: dp: 8 (over x, y_lo), fsdp: 16 (over z, core), tensor: 2 (over y_hi).
Axes of the slice: x: 4, y: 4 (y_hi: 2, y_lo: 2; y = y_hi * 2 + y_lo), z: 8, core: 2. Of those that a mesh axis runs over, the one named last changes fastest.
Arguments:
- pooled: bfloat16 [8, 3072, 1152], P('dp', 'fsdp'), may hold values from -6 to 6
- ln_gain: float32 [1152], replicated, may hold values from 0.5 to 1.5
- w_in: bfloat16 [1152, 4304], P('fsdp', 'tensor'), may hold values from -0.1875 to 0.1875
- w_out: bfloat16 [4304, 1152], P('tensor', 'fsdp'), may hold values from -0.09375 to 0.09375
- texts: bfloat16 [8, 3072, 1152], P('dp', ('fsdp', 'tensor')), may hold values from -6 to 6
Outputs:
- grad_pooled: float32 [8, 3072, 1152], P('dp', 'fsdp')
- grad_in: float32 [1152, 4304], P('fsdp', 'tensor')
- grad_out: float32 [4304, 1152], P('tensor', 'fsdp')
All inputs are finite; a program needn't handle non-finite values.
Results may differ from a plain program's by a relative error of at most 0.022.
Values may be sent and summed in bfloat16 or wider, within the bound.
A program may use at most 64 MiB of HBM per device.

v0:
```python
import jax
import jax.numpy as jnp
from jax import lax
from jax.sharding import PartitionSpec as P

ln_eps = 1e-06
norm_eps = 1e-06
logit_scale = 10.0
logit_bias = -2.0


def passed_along(block, axis, distance):
    devices = range(lax.axis_size(axis))
    route = [((i - distance) % len(devices), i) for i in devices]
    return lax.ppermute(block, axis, route)


def gelu_tanh(values):
    return jax.nn.gelu(values, approximate=True)


def unit_rows(values):
    return values / jnp.sqrt(jnp.sum(values * values, axis=-1, keepdims=True) + norm_eps)


def text_columns(first, number, block_rows, offset, stride):
    places = first + jnp.arange(number, dtype=jnp.int32)
    return places // block_rows * stride + offset + places % block_rows


def body(pooled, ln_gain, w_in, w_out, texts):
    rows = pooled[0].astype(jnp.float32)
    images = rows.shape[0]
    width = rows.shape[1]
    row_mean = jnp.mean(rows, axis=1, keepdims=True)
    centred = rows - row_mean
    inv_std = lax.rsqrt(jnp.mean(centred * centred, axis=1, keepdims=True) + ln_eps)
    normal_rows = centred * inv_std
    unit_in = (normal_rows * ln_gain).astype(jnp.bfloat16)
    full_in = lax.all_gather(w_in, "fsdp", axis=0, tiled=True)
    pre_act = jnp.dot(unit_in, full_in, preferred_element_type=jnp.float32)
    hidden = gelu_tanh(pre_act).astype(jnp.bfloat16)
    full_out = lax.all_gather(w_out, "fsdp", axis=1, tiled=True)
    partial_mix = jnp.dot(hidden, full_out, preferred_element_type=jnp.float32)
    mixed = rows + lax.psum(partial_mix.astype(jnp.bfloat16), "tensor").astype(jnp.float32)
    row_norm = jnp.sqrt(jnp.sum(mixed * mixed, axis=1, keepdims=True) + norm_eps)
    image_unit = mixed / row_norm
    image_b = image_unit.astype(jnp.bfloat16)
    text_b = unit_rows(texts[0].astype(jnp.float32)).astype(jnp.bfloat16)
    cycle_index = lax.axis_index("fsdp")
    cycle_size = lax.axis_size("fsdp")
    image_places = cycle_index * images + jnp.arange(images, dtype=jnp.int32)
    offset = lax.axis_index("tensor") * text_b.shape[0]
    block_rows = text_b.shape[0]

    def score_block(running, block, columns):
        logits = (
            logit_scale
            * jnp.einsum("rd,cd->rc", image_b, block, preferred_element_type=jnp.float32)
            + logit_bias
        )
        match = (image_places[:, None] == columns[None, :]).astype(jnp.float32)
        weights = (jax.nn.sigmoid(logits) - match).astype(jnp.bfloat16)
        return running + jnp.dot(weights, block, preferred_element_type=jnp.float32)

    def source_columns(source):
        return text_columns(source * block_rows, block_rows, block_rows, offset, images)

    empty = jnp.zeros((images, width), jnp.float32)
    running = score_block(empty, text_b, source_columns(cycle_index))

    def cycle_turn(turn, carry):
        total, moving = carry
        moving = passed_along(moving, "fsdp", 1)
        total = score_block(total, moving, source_columns((cycle_index - turn) % cycle_size))
        return (total, moving)

    running, _ = lax.fori_loop(1, cycle_size, cycle_turn, (running, text_b))
    grad_unit = logit_scale * running
    grad_unit = lax.psum(grad_unit.astype(jnp.bfloat16), "tensor").astype(jnp.float32)
    grad_mixed = (
        grad_unit - image_unit * jnp.sum(image_unit * grad_unit, axis=1, keepdims=True)
    ) / row_norm
    grad_b = grad_mixed.astype(jnp.bfloat16)
    grad_hidden = jnp.einsum("rd,fd->rf", grad_b, full_out, preferred_element_type=jnp.float32)
    _, gelu_back = jax.vjp(gelu_tanh, pre_act)
    grad_pre = gelu_back(grad_hidden)[0].astype(jnp.bfloat16)
    partial_unit = jnp.einsum("rf,df->rd", grad_pre, full_in, preferred_element_type=jnp.float32)
    grad_unit_in = lax.psum(partial_unit.astype(jnp.bfloat16), "tensor").astype(jnp.float32)
    scaled = grad_unit_in * ln_gain
    grad_rows = inv_std * (
        scaled
        - jnp.mean(scaled, axis=1, keepdims=True)
        - normal_rows * jnp.mean(scaled * normal_rows, axis=1, keepdims=True)
    )
    grad_pooled = (grad_mixed + grad_rows)[None]
    grad_in_part = lax.psum_scatter(
        jnp.einsum("rd,rf->df", unit_in, grad_pre, preferred_element_type=jnp.float32).astype(
            jnp.bfloat16
        ),
        "fsdp",
        scatter_dimension=0,
        tiled=True,
    )
    out_term = jnp.einsum("rf,rd->fd", hidden, grad_b, preferred_element_type=jnp.float32)
    grad_out_part = lax.psum_scatter(
        out_term.astype(jnp.bfloat16), "fsdp", scatter_dimension=1, tiled=True
    )
    grad_in, grad_out = (
        lax.psum(grad_in_part, "dp").astype(jnp.float32),
        lax.psum(grad_out_part, "dp").astype(jnp.float32),
    )
    return (grad_pooled, grad_in, grad_out)


def solution(mesh):
    placed = (
        P("dp", "fsdp", None),
        P(),
        P("fsdp", "tensor"),
        P("tensor", "fsdp"),
        P("dp", ("fsdp", "tensor"), None),
    )
    return jax.shard_map(
        body,
        mesh=mesh,
        in_specs=placed,
        out_specs=(P("dp", "fsdp", None), P("fsdp", "tensor"), P("tensor", "fsdp")),
        check_vma=False,
    )
```

profile of v0, /device:TPU:32, one launch (start us, length us, event | category | flops | bytes accessed | tf_op | source)
XLA Modules:
  0.0 573.5 jit_solution(10789957357336990693)
XLA Ops:
  7.2 0.7 all-gather.3.cloned.1.call-update
  8.0 0.7 all-gather.5.cloned.1.call-update
  8.8 1.1 fusion.53
  9.8 1.2 convert_reduce_fusion
  11.0 1.3 fusion.48
  12.3 42.3 %all-gather.3.cloned.1.call-done = bf16[1152,2152]{1,0:T(8,128)(2,1)} async-done(((bf16[72,2152]{1,0:T(8,128)(2,1)}), bf16[1152,2152]{1,0:T(8,128)(2,1)}) %all-gather.3.cloned.1.call-update) | async-done | bytes 4958224 | tf_op jit(solution)/shard_map/all_gather | solution.py:40
  54.6 3.8 fusion.72
  58.5 39.3 %all-gather.5.cloned.1.call-done = bf16[2152,1152]{0,1:T(8,128)(2,1)} async-done(((bf16[2152,72]{0,1:T(8,128)(2,1)}), bf16[2152,1152]{0,1:T(8,128)(2,1)}) %all-gather.5.cloned.1.call-update) | async-done | bytes 4958224 | tf_op jit(solution)/shard_map/all_gather | solution.py:43
  97.7 4.9 convolution_convert_fusion.3
  102.8 39.1 %all-reduce.8.cloned.1.call-done = bf16[192,1152]{1,0:T(8,128)(2,1)} async-done(((bf16[192,1152]{1,0:T(8,128)(2,1)}), bf16[192,1152]{1,0:T(8,128)(2,1)}) %all-reduce.8.cloned.1.call-update) | async-done | bytes 442384 | tf_op jit(solution)/shard_map/psum | solution.py:45
  142.0 1.2 multiply_reduce_fusion
  143.2 1.2 fusion.74
  145.0 101.4 %while.19 = (s32[]{:T(128)}, f32[192,1152]{1,0:T(8,128)S(1)}, bf16[96,1152]{1,0:T(8,128)(2,1)S(1)}, bf16[192,1152]{1,0:T(8,128)(2,1)S(1)}, s32[]{:T(128)}, /*ind...) while((s32[]{:T(128)}, f32[192,1152]{1,0:T(8,128)S(1)}, ...), condition=%wide.region_6.7_spmd.clone, body=%wide.region_5.6_spmd.clone.sunk | while | flops 85323472 | bytes 3762734 | solution.py:78
  145.1 5.3 collective-permute-done
  151.2 5.3 collective-permute-done
  157.3 5.3 collective-permute-done
  163.4 5.3 collective-permute-done
  169.4 5.3 collective-permute-done
  175.5 5.3 collective-permute-done
  180.8 0.7 convolution_add_fusion.2
  181.6 5.8 %collective-permute-done = bf16[96,1152]{1,0:T(8,128)(2,1)S(1)} collective-permute-done((bf16[96,1152]{1,0:T(8,128)(2,1)S(1)}, bf16[96,1152]{1,0:T(8,128)(2,1)S(1)}, u32[]{:S(2)}, u32[]{:S(2)}) %collective-permute-start) | collective-permute-done | bytes 221216 | tf_op jit(solution)/shard_map/while/body/eval_jaxpr/ppermute | solution.py:15
  188.2 6.5 %collective-permute-done = bf16[96,1152]{1,0:T(8,128)(2,1)S(1)} collective-permute-done((bf16[96,1152]{1,0:T(8,128)(2,1)S(1)}, bf16[96,1152]{1,0:T(8,128)(2,1)S(1)}, u32[]{:S(2)}, u32[]{:S(2)}) %collective-permute-start) | collective-permute-done | bytes 221216 | tf_op jit(solution)/shard_map/while/body/eval_jaxpr/ppermute | solution.py:15
  194.7 0.7 convolution_add_fusion.2
  195.5 6.5 %collective-permute-done = bf16[96,1152]{1,0:T(8,128)(2,1)S(1)} collective-permute-done((bf16[96,1152]{1,0:T(8,128)(2,1)S(1)}, bf16[96,1152]{1,0:T(8,128)(2,1)S(1)}, u32[]{:S(2)}, u32[]{:S(2)}) %collective-permute-start) | collective-permute-done | bytes 221216 | tf_op jit(solution)/shard_map/while/body/eval_jaxpr/ppermute | solution.py:15
  202.8 6.5 %collective-permute-done = bf16[96,1152]{1,0:T(8,128)(2,1)S(1)} collective-permute-done((bf16[96,1152]{1,0:T(8,128)(2,1)S(1)}, bf16[96,1152]{1,0:T(8,128)(2,1)S(1)}, u32[]{:S(2)}, u32[]{:S(2)}) %collective-permute-start) | collective-permute-done | bytes 221216 | tf_op jit(solution)/shard_map/while/body/eval_jaxpr/ppermute | solution.py:15
  209.3 0.7 convolution_add_fusion.2
  210.1 6.5 %collective-permute-done = bf16[96,1152]{1,0:T(8,128)(2,1)S(1)} collective-permute-done((bf16[96,1152]{1,0:T(8,128)(2,1)S(1)}, bf16[96,1152]{1,0:T(8,128)(2,1)S(1)}, u32[]{:S(2)}, u32[]{:S(2)}) %collective-permute-start) | collective-permute-done | bytes 221216 | tf_op jit(solution)/shard_map/while/body/eval_jaxpr/ppermute | solution.py:15
  217.4 6.5 %collective-permute-done = bf16[96,1152]{1,0:T(8,128)(2,1)S(1)} collective-permute-done((bf16[96,1152]{1,0:T(8,128)(2,1)S(1)}, bf16[96,1152]{1,0:T(8,128)(2,1)S(1)}, u32[]{:S(2)}, u32[]{:S(2)}) %collective-permute-start) | collective-permute-done | bytes 221216 | tf_op jit(solution)/shard_map/while/body/eval_jaxpr/ppermute | solution.py:15
  223.9 0.7 convolution_add_fusion.2
  224.7 6.5 %collective-permute-done = bf16[96,1152]{1,0:T(8,128)(2,1)S(1)} collective-permute-done((bf16[96,1152]{1,0:T(8,128)(2,1)S(1)}, bf16[96,1152]{1,0:T(8,128)(2,1)S(1)}, u32[]{:S(2)}, u32[]{:S(2)}) %collective-permute-start) | collective-permute-done | bytes 221216 | tf_op jit(solution)/shard_map/while/body/eval_jaxpr/ppermute | solution.py:15
  232.0 6.5 %collective-permute-done = bf16[96,1152]{1,0:T(8,128)(2,1)S(1)} collective-permute-done((bf16[96,1152]{1,0:T(8,128)(2,1)S(1)}, bf16[96,1152]{1,0:T(8,128)(2,1)S(1)}, u32[]{:S(2)}, u32[]{:S(2)}) %collective-permute-start) | collective-permute-done | bytes 221216 | tf_op jit(solution)/shard_map/while/body/eval_jaxpr/ppermute | solution.py:15
  239.3 6.5 %collective-permute-done = bf16[96,1152]{1,0:T(8,128)(2,1)S(1)} collective-permute-done((bf16[96,1152]{1,0:T(8,128)(2,1)S(1)}, bf16[96,1152]{1,0:T(8,128)(2,1)S(1)}, u32[]{:S(2)}, u32[]{:S(2)}) %collective-permute-start) | collective-permute-done | bytes 221216 | tf_op jit(solution)/shard_map/while/body/eval_jaxpr/ppermute | solution.py:15
  246.5 0.8 multiply_convert_fusion.1
  247.4 47.6 %all-reduce.10.cloned.1.call-done = bf16[192,1152]{1,0:T(8,128)(2,1)} async-done(((bf16[192,1152]{1,0:T(8,128)(2,1)}), bf16[192,1152]{1,0:T(8,128)(2,1)}) %all-reduce.10.cloned.1.call-update) | async-done | bytes 442384 | tf_op jit(solution)/shard_map/psum | solution.py:80
  294.9 1.5 fusion.49
  296.4 4.7 fusion.26
  301.2 2.4 convolution_convert_fusion.2
  303.7 3.9 convolution_convert_fusion.1
  307.9 0.8 copy-done.3
  308.6 4.1 convolution_convert_fusion
  312.8 30.4 %all-reduce.12.cloned.1.call-done = bf16[192,1152]{1,0:T(8,128)(2,1)} async-done(((bf16[192,1152]{1,0:T(8,128)(2,1)}), bf16[192,1152]{1,0:T(8,128)(2,1)}) %all-reduce.12.cloned.1.call-update) | async-done | bytes 442384 | tf_op jit(solution)/shard_map/psum | solution.py:89
  343.3 1.4 fusion.51
  344.7 64.2 %reduce-scatter.7.cloned.1.call-done = bf16[72,2152]{1,0:T(8,128)(2,1)} async-done(((bf16[1152,2152]{1,0:T(8,128)(2,1)}), bf16[72,2152]{1,0:T(8,128)(2,1)}) %reduce-scatter.7.cloned.1.call-update) | async-done | bytes 309904
  408.9 68.5 %reduce-scatter.9.cloned.1.call-done = bf16[2152,72]{0,1:T(8,128)(2,1)} async-done(((bf16[2152,1152]{0,1:T(8,128)(2,1)}), bf16[2152,72]{0,1:T(8,128)(2,1)}) %reduce-scatter.9.cloned.1.call-update) | async-done | bytes 309904
  477.4 1.5 fusion.47
  478.9 84.1 %all-reduce.14.cloned.1.call-done = (bf16[72,2152]{1,0:T(8,128)(2,1)}, bf16[2152,72]{0,1:T(8,128)(2,1)}) async-done(((bf16[72,2152]{1,0:T(8,128)(2,1)}, bf16[2152,72]{0,1:T(8,128)(2,1)}), (bf16[72,2152]{1,0:T(8,128)(2,1)}, bf16[2152,72]{0,1:T(8,128)(2,1)})) %all-reduce.14.cloned.1.call-update) | async-done | bytes 619792 | tf_op jit(solution)/shard_map/psum | solution.py:110
  563.0 1.8 convert_element_type.107
  564.9 1.8 convert_element_type.109
  (114 shorter events, 9.8 us)
Async XLA Ops:
  7.2 47.5 %copy-start = (bf16[1,192,1152]{2,1,0:T(8,128)(2,1)S(1)}, bf16[1,192,1152]{2,1,0:T(8,128)(2,1)}, u32[]{:S(2)}) copy-start(bf16[1,192,1152]{2,1,0:T(8,128)(2,1)} %param.7) | copy-start | bytes 1327108
  7.2 47.5 %copy-start.7 = (f32[1152]{0:T(1024)S(1)}, f32[1152]{0:T(1024)}, u32[]{:S(2)}) copy-start(f32[1152]{0:T(1024)} %param.8) | copy-start | bytes 13828
  7.2 47.4 %all-gather.3.cloned.1.call-start = ((), (), s32[]{:S(2)}) async-start(), calls=%async_computation.2 | async-start | bytes 5326848 | tf_op jit(solution)/shard_map/all_gather | solution.py:40
  7.9 89.8 %all-gather.5.cloned.1.call-start = ((), (), s32[]{:S(2)}) async-start(), calls=%async_computation.3 | async-start | bytes 5326848 | tf_op jit(solution)/shard_map/all_gather | solution.py:43
  8.7 133.3 %all-reduce.8.cloned.1.call-start = ((), (), s32[]{:S(2)}) async-start(), calls=%async_computation.4 | async-start | bytes 884736 | tf_op jit(solution)/shard_map/psum | solution.py:45
  58.4 44.2 %copy-start.4 = (f32[192,2152]{1,0:T(8,128)}, f32[192,2152]{1,0:T(8,128)S(1)}, u32[]{:S(2)}) copy-start(f32[192,2152]{1,0:T(8,128)S(1)} %fusion.72) | copy-start | bytes 4958212
  58.5 44.2 %copy-start.6 = (bf16[1,96,1152]{2,1,0:T(8,128)(2,1)S(1)}, bf16[1,96,1152]{2,1,0:T(8,128)(2,1)}, u32[]{:S(2)}) copy-start(bf16[1,96,1152]{2,1,0:T(8,128)(2,1)} %param.11) | copy-start | bytes 663556
  102.6 192.3 %all-reduce.10.cloned.1.call-start = ((), (), s32[]{:S(2)}) async-start(), calls=%async_computation.5 | async-start | bytes 884736 | tf_op jit(solution)/shard_map/psum | solution.py:80
  145.0 5.4 collective-permute-start
  151.1 5.4 collective-permute-start
  157.2 5.4 collective-permute-start
  163.3 5.4 collective-permute-start
  169.4 5.4 collective-permute-start
  175.4 5.4 collective-permute-start
  181.5 5.9 %collective-permute-start = (bf16[96,1152]{1,0:T(8,128)(2,1)S(1)}, bf16[96,1152]{1,0:T(8,128)(2,1)S(1)}, u32[]{:S(2)}, u32[]{:S(2)}) collective-permute-start(bf16[96,1152]{1,0:T(8,128)(2,1)S(1)} %get-tuple-element.306), channel_id=1, source_target_pairs={{30,0},{0,2},{2,4},{4,6},{6,8},{8,10},{10,12},{12,14},{14,16},{16,... | collective-permute-start | bytes 663560 | tf_op jit(solution)/shard_map/while/body/eval_jaxpr/ppermute | solution.py:15
  188.1 6.6 %collective-permute-start = (bf16[96,1152]{1,0:T(8,128)(2,1)S(1)}, bf16[96,1152]{1,0:T(8,128)(2,1)S(1)}, u32[]{:S(2)}, u32[]{:S(2)}) collective-permute-start(bf16[96,1152]{1,0:T(8,128)(2,1)S(1)} %get-tuple-element.306), channel_id=1, source_target_pairs={{30,0},{0,2},{2,4},{4,6},{6,8},{8,10},{10,12},{12,14},{14,16},{16,... | collective-permute-start | bytes 663560 | tf_op jit(solution)/shard_map/while/body/eval_jaxpr/ppermute | solution.py:15
  195.4 6.6 %collective-permute-start = (bf16[96,1152]{1,0:T(8,128)(2,1)S(1)}, bf16[96,1152]{1,0:T(8,128)(2,1)S(1)}, u32[]{:S(2)}, u32[]{:S(2)}) collective-permute-start(bf16[96,1152]{1,0:T(8,128)(2,1)S(1)} %get-tuple-element.306), channel_id=1, source_target_pairs={{30,0},{0,2},{2,4},{4,6},{6,8},{8,10},{10,12},{12,14},{14,16},{16,... | collective-permute-start | bytes 663560 | tf_op jit(solution)/shard_map/while/body/eval_jaxpr/ppermute | solution.py:15
  202.7 6.6 %collective-permute-start = (bf16[96,1152]{1,0:T(8,128)(2,1)S(1)}, bf16[96,1152]{1,0:T(8,128)(2,1)S(1)}, u32[]{:S(2)}, u32[]{:S(2)}) collective-permute-start(bf16[96,1152]{1,0:T(8,128)(2,1)S(1)} %get-tuple-element.306), channel_id=1, source_target_pairs={{30,0},{0,2},{2,4},{4,6},{6,8},{8,10},{10,12},{12,14},{14,16},{16,... | collective-permute-start | bytes 663560 | tf_op jit(solution)/shard_map/while/body/eval_jaxpr/ppermute | solution.py:15
  210.0 6.6 %collective-permute-start = (bf16[96,1152]{1,0:T(8,128)(2,1)S(1)}, bf16[96,1152]{1,0:T(8,128)(2,1)S(1)}, u32[]{:S(2)}, u32[]{:S(2)}) collective-permute-start(bf16[96,1152]{1,0:T(8,128)(2,1)S(1)} %get-tuple-element.306), channel_id=1, source_target_pairs={{30,0},{0,2},{2,4},{4,6},{6,8},{8,10},{10,12},{12,14},{14,16},{16,... | collective-permute-start | bytes 663560 | tf_op jit(solution)/shard_map/while/body/eval_jaxpr/ppermute | solution.py:15
  217.3 6.6 %collective-permute-start = (bf16[96,1152]{1,0:T(8,128)(2,1)S(1)}, bf16[96,1152]{1,0:T(8,128)(2,1)S(1)}, u32[]{:S(2)}, u32[]{:S(2)}) collective-permute-start(bf16[96,1152]{1,0:T(8,128)(2,1)S(1)} %get-tuple-element.306), channel_id=1, source_target_pairs={{30,0},{0,2},{2,4},{4,6},{6,8},{8,10},{10,12},{12,14},{14,16},{16,... | collective-permute-start | bytes 663560 | tf_op jit(solution)/shard_map/while/body/eval_jaxpr/ppermute | solution.py:15
  224.6 6.6 %collective-permute-start = (bf16[96,1152]{1,0:T(8,128)(2,1)S(1)}, bf16[96,1152]{1,0:T(8,128)(2,1)S(1)}, u32[]{:S(2)}, u32[]{:S(2)}) collective-permute-start(bf16[96,1152]{1,0:T(8,128)(2,1)S(1)} %get-tuple-element.306), channel_id=1, source_target_pairs={{30,0},{0,2},{2,4},{4,6},{6,8},{8,10},{10,12},{12,14},{14,16},{16,... | collective-permute-start | bytes 663560 | tf_op jit(solution)/shard_map/while/body/eval_jaxpr/ppermute | solution.py:15
  231.9 6.6 %collective-permute-start = (bf16[96,1152]{1,0:T(8,128)(2,1)S(1)}, bf16[96,1152]{1,0:T(8,128)(2,1)S(1)}, u32[]{:S(2)}, u32[]{:S(2)}) collective-permute-start(bf16[96,1152]{1,0:T(8,128)(2,1)S(1)} %get-tuple-element.306), channel_id=1, source_target_pairs={{30,0},{0,2},{2,4},{4,6},{6,8},{8,10},{10,12},{12,14},{14,16},{16,... | collective-permute-start | bytes 663560 | tf_op jit(solution)/shard_map/while/body/eval_jaxpr/ppermute | solution.py:15
  239.2 6.6 %collective-permute-start = (bf16[96,1152]{1,0:T(8,128)(2,1)S(1)}, bf16[96,1152]{1,0:T(8,128)(2,1)S(1)}, u32[]{:S(2)}, u32[]{:S(2)}) collective-permute-start(bf16[96,1152]{1,0:T(8,128)(2,1)S(1)} %get-tuple-element.306), channel_id=1, source_target_pairs={{30,0},{0,2},{2,4},{4,6},{6,8},{8,10},{10,12},{12,14},{14,16},{16,... | collective-permute-start | bytes 663560 | tf_op jit(solution)/shard_map/while/body/eval_jaxpr/ppermute | solution.py:15
  246.5 48.5 %copy-start.1 = (bf16[192,1152]{1,0:T(8,128)(2,1)S(1)}, bf16[192,1152]{1,0:T(8,128)(2,1)}, u32[]{:S(2)}) copy-start(bf16[192,1152]{1,0:T(8,128)(2,1)} %all-reduce.8.cloned.1.call-done) | copy-start | bytes 1327108
  246.5 49.9 %copy-start.5 = (f32[192,2152]{1,0:T(8,128)S(1)}, f32[192,2152]{1,0:T(8,128)}, u32[]{:S(2)}) copy-start(f32[192,2152]{1,0:T(8,128)} %copy-done.4) | copy-start | bytes 4958212
  247.3 95.9 %all-reduce.12.cloned.1.call-start = ((), (), s32[]{:S(2)}) async-start(), calls=%async_computation.6 | async-start | bytes 884736 | tf_op jit(solution)/shard_map/psum | solution.py:89
  294.9 6.2 %slice-start = ((s8[5013504]{0:T(1024)(128)(4,1)}), s8[4194304]{0:T(1024)(128)(4,1)S(1)}, s32[]{:S(2)}) async-start(s8[5013504]{0:T(1024)(128)(4,1)} %bitcast.75), calls=%async_computation.10 | async-start | bytes 8388608
  296.4 4.8 slice-start.1
  303.6 105.3 %reduce-scatter.7.cloned.1.call-start = ((), (), s32[]{:S(2)}) async-start(), calls=%async_computation.7 | async-start | bytes 5326848
  307.6 1.0 copy-start.3
  307.6 169.8 %reduce-scatter.9.cloned.1.call-start = ((), (), s32[]{:S(2)}) async-start(), calls=%async_computation.8 | async-start | bytes 5326848
  312.8 250.3 %all-reduce.14.cloned.1.call-start = ((), (), s32[]{:S(2)}) async-start(), calls=%async_computation.9 | async-start | bytes 1253376 | tf_op jit(solution)/shard_map/psum | solution.py:110
  343.3 134.2 %copy-start.2 = (bf16[192,1152]{1,0:T(8,128)(2,1)S(1)}, bf16[192,1152]{1,0:T(8,128)(2,1)}, u32[]{:S(2)}) copy-start(bf16[192,1152]{1,0:T(8,128)(2,1)} %all-reduce.12.cloned.1.call-done) | copy-start | bytes 1327108
Sparse Core Ops, SparseCore 0:
  9.8 44.7 all-gather.2
  56.5 41.2 all-gather.4
  102.8 39.1 all-reduce.7
  247.4 47.4 all-reduce.9
  303.7 39.4 all-reduce.11
  345.7 63.1 reduce-scatter.6
  411.5 65.8 reduce-scatter.8
  480.1 82.8 all-reduce.13
where the time goes:
time: 574 us
  waiting for transfers between devices  507 us (88%)
  matrix products  34.6 us (6%)
  other arithmetic  15.3 us (3%)
  between operations  14.3 us (2%)
    unnamed x10, waiting for transfers between devices  134 us
    ppermute x15, waiting for transfers between devices, passed_along(): return lax.ppermute(block, axis, route)  89.5 us
    psum x1, waiting for transfers between devices, body(): lax.psum(grad_in_part, 'dp').astype(jnp.float32)  84.1 us
    psum x1, waiting for transfers between devices, body(): lax.psum(grad_unit.astype(jnp.bfloat16), 'tensor').astype(jnp.float32)  47.6 us
    all_gather x1, waiting for transfers between devices, body(): full_in = lax.all_gather(w_in, 'fsdp', axis=0, tiled=True)  42.3 us
    all_gather x1, waiting for transfers between devices, body(): full_out = lax.all_gather(w_out, 'fsdp', axis=1, tiled=True)  39.3 us
    psum x1, waiting for transfers between devices, body(): lax.psum(partial_mix.astype(jnp.bfloat16), 'tensor').astype(jnp.float32)  39.1 us
    psum x1, waiting for transfers between devices, body(): lax.psum(partial_unit.astype(jnp.bfloat16), 'tensor').astype(jnp.float32)  30.4 us
  transfers between devices with their start and end apart: 23, of which 23 were waited for; matrix products, arithmetic and copies ran while one was open for 3% of the time, Pallas kernels for 0%

commit v1 on v0

v1 whole, which is shorter than its diff:
```python
import jax
import jax.numpy as jnp
from jax import lax
from jax.sharding import PartitionSpec as P

ln_eps = 1e-06
norm_eps = 1e-06
logit_scale = 10.0
logit_bias = -2.0


def passed_along(block, axis, distance):
    devices = range(lax.axis_size(axis))
    route = [((i - distance) % len(devices), i) for i in devices]
    return lax.ppermute(block, axis, route)


def swapped_sum(partial, axis):
    mine = partial.astype(jnp.bfloat16)
    other = lax.ppermute(mine, axis, [(0, 1), (1, 0)])
    return mine.astype(jnp.float32) + other.astype(jnp.float32)


def doubling_sum(parts, axis):
    size = lax.axis_size(axis)
    mine = [p.astype(jnp.bfloat16) for p in parts]
    totals = None
    bit = 1
    while bit < size:
        route = [(i, i ^ bit) for i in range(size)]
        others = [lax.ppermute(m, axis, route) for m in mine]
        totals = [m.astype(jnp.float32) + o.astype(jnp.float32) for m, o in zip(mine, others)]
        mine = [t.astype(jnp.bfloat16) for t in totals]
        bit *= 2
    return totals


def gelu_tanh(values):
    return jax.nn.gelu(values, approximate=True)


def unit_rows(values):
    return values / jnp.sqrt(jnp.sum(values * values, axis=-1, keepdims=True) + norm_eps)


def text_columns(first, number, block_rows, offset, stride):
    places = first + jnp.arange(number, dtype=jnp.int32)
    return places // block_rows * stride + offset + places % block_rows


def body(pooled, ln_gain, w_in, w_out, texts):
    rows = pooled[0].astype(jnp.float32)
    images = rows.shape[0]
    width = rows.shape[1]
    text_b = unit_rows(texts[0].astype(jnp.float32)).astype(jnp.bfloat16)
    cycle_index = lax.axis_index("fsdp")
    cycle_size = lax.axis_size("fsdp")
    offset = lax.axis_index("tensor") * text_b.shape[0]
    block_rows = text_b.shape[0]

    def source_columns(source):
        return text_columns(source * block_rows, block_rows, block_rows, offset, images)

    blocks = [text_b]
    sources = [cycle_index]
    ahead = text_b
    for step in range(1, cycle_size // 2 + 1):
        ahead = passed_along(ahead, "fsdp", 1)
        blocks.append(ahead)
        sources.append((cycle_index - step) % cycle_size)
    behind = text_b
    for step in range(1, (cycle_size - 1) // 2 + 1):
        behind = passed_along(behind, "fsdp", -1)
        blocks.append(behind)
        sources.append((cycle_index + step) % cycle_size)
    all_texts = jnp.concatenate(blocks, axis=0)
    columns = jnp.concatenate([source_columns(s) for s in sources], axis=0)

    row_mean = jnp.mean(rows, axis=1, keepdims=True)
    centred = rows - row_mean
    inv_std = lax.rsqrt(jnp.mean(centred * centred, axis=1, keepdims=True) + ln_eps)
    normal_rows = centred * inv_std
    unit_in = (normal_rows * ln_gain).astype(jnp.bfloat16)
    full_in = lax.all_gather(w_in, "fsdp", axis=0, tiled=True)
    pre_act = jnp.dot(unit_in, full_in, preferred_element_type=jnp.float32)
    hidden = gelu_tanh(pre_act).astype(jnp.bfloat16)
    full_out = lax.all_gather(w_out, "fsdp", axis=1, tiled=True)
    partial_mix = jnp.dot(hidden, full_out, preferred_element_type=jnp.float32)
    mixed = rows + swapped_sum(partial_mix, "tensor")
    row_norm = jnp.sqrt(jnp.sum(mixed * mixed, axis=1, keepdims=True) + norm_eps)
    image_unit = mixed / row_norm
    image_b = image_unit.astype(jnp.bfloat16)
    image_places = cycle_index * images + jnp.arange(images, dtype=jnp.int32)

    logits = (
        logit_scale
        * jnp.einsum("rd,cd->rc", image_b, all_texts, preferred_element_type=jnp.float32)
        + logit_bias
    )
    match = (image_places[:, None] == columns[None, :]).astype(jnp.float32)
    weights = (jax.nn.sigmoid(logits) - match).astype(jnp.bfloat16)
    running = jnp.dot(weights, all_texts, preferred_element_type=jnp.float32)
    grad_unit = swapped_sum(logit_scale * running, "tensor")
    grad_mixed = (
        grad_unit - image_unit * jnp.sum(image_unit * grad_unit, axis=1, keepdims=True)
    ) / row_norm
    grad_b = grad_mixed.astype(jnp.bfloat16)
    grad_hidden = jnp.einsum("rd,fd->rf", grad_b, full_out, preferred_element_type=jnp.float32)
    _, gelu_back = jax.vjp(gelu_tanh, pre_act)
    grad_pre = gelu_back(grad_hidden)[0].astype(jnp.bfloat16)
    partial_unit = jnp.einsum("rf,df->rd", grad_pre, full_in, preferred_element_type=jnp.float32)
    grad_unit_in = swapped_sum(partial_unit, "tensor")
    scaled = grad_unit_in * ln_gain
    grad_rows = inv_std * (
        scaled
        - jnp.mean(scaled, axis=1, keepdims=True)
        - normal_rows * jnp.mean(scaled * normal_rows, axis=1, keepdims=True)
    )
    grad_pooled = (grad_mixed + grad_rows)[None]
    grad_in_part = lax.psum_scatter(
        jnp.einsum("rd,rf->df", unit_in, grad_pre, preferred_element_type=jnp.float32).astype(
            jnp.bfloat16
        ),
        "fsdp",
        scatter_dimension=0,
        tiled=True,
    )
    out_term = jnp.einsum("rf,rd->fd", hidden, grad_b, preferred_element_type=jnp.float32)
    grad_out_part = lax.psum_scatter(
        out_term.astype(jnp.bfloat16), "fsdp", scatter_dimension=1, tiled=True
    )
    grad_in, grad_out = doubling_sum([grad_in_part, grad_out_part], "dp")
    return (grad_pooled, grad_in, grad_out)


def solution(mesh):
    placed = (
        P("dp", "fsdp", None),
        P(),
        P("fsdp", "tensor"),
        P("tensor", "fsdp"),
        P("dp", ("fsdp", "tensor"), None),
    )
    return jax.shard_map(
        body,
        mesh=mesh,
        in_specs=placed,
        out_specs=(P("dp", "fsdp", None), P("fsdp", "tensor"), P("tensor", "fsdp")),
        check_vma=False,
    )
```

time: 574 us -> 326 us (0.57)
  waiting for transfers between devices: 507 us -> 211 us
  starting transfers between devices: 0.78 us -> 42.8 us
  local copies, waits for them, and re-layouts: 1.07 us -> 13.9 us
    psum x4 -> x0, waiting for transfers between devices: 201 us -> none  [the longest x1 84.1 us: body(): lax.psum(grad_in_part, 'dp').astype(jnp.float32)]
    ppermute x15, waiting for transfers between devices: 89.5 us -> 30.1 us  [passed_along(): return lax.ppermute(block, axis, route)]
    ppermute x0 -> x9, waiting for transfers between devices: none -> 47.9 us  [the longest x3 28.5 us: swapped_sum(): other = lax.ppermute(mine, axis, [(0, 1), (1, 0)])]
    all_gather x1, waiting for transfers between devices: 42.3 us -> 0.01 us  [body(): full_in = lax.all_gather(w_in, 'fsdp', axis=0, tiled=True)]
    unnamed x10 -> x6, waiting for transfers between devices: 134 us -> 106 us
    ppermute x0 -> x9, starting transfers between devices: none -> 22.1 us  [the longest x6 12.1 us: doubling_sum(): others = [lax.ppermute(m, axis, route) for m in mine]]
    ppermute x15, starting transfers between devices: 0.28 us -> 20.3 us  [passed_along(): return lax.ppermute(block, axis, route)]
    all_gather x1, waiting for transfers between devices: 39.3 us -> 26.3 us  [body(): full_out = lax.all_gather(w_out, 'fsdp', axis=1, tiled=True)]
  transfers between devices with their start and end apart: 23 -> 28, of which waited for: 23 -> 21; matrix products, arithmetic and copies ran while one was open for 3% -> 11% of each run, Pallas kernels for 0% -> 0%
where the time goes in v1:
time: 326 us; the launch traced here: 323 us
  waiting for transfers between devices  211 us (65%)
  starting transfers between devices  42.8 us (13%)
  matrix products  29.7 us (9%)
  local copies, waits for them, and re-layouts  13.9 us (4%)
  between operations  13.9 us (4%)
  other arithmetic  12.2 us (4%)
    unnamed x6, waiting for transfers between devices  106 us
    ppermute x15, waiting for transfers between devices, passed_along(): return lax.ppermute(block, axis, route)  30.1 us
    ppermute x3, waiting for transfers between devices, swapped_sum(): other = lax.ppermute(mine, axis, [(0, 1), (1, 0)])  28.5 us
    all_gather x1, waiting for transfers between devices, body(): full_out = lax.all_gather(w_out, 'fsdp', axis=1, tiled=True)  26.3 us
    ppermute x15, starting transfers between devices, passed_along(): return lax.ppermute(block, axis, route)  20.3 us
    ppermute x6, waiting for transfers between devices, doubling_sum(): others = [lax.ppermute(m, axis, route) for m in mine]  19.4 us
    unnamed x28, local copies, waits for them, and re-layouts  13.1 us
    ppermute x6, starting transfers between devices, doubling_sum(): others = [lax.ppermute(m, axis, route) for m in mine]  12.1 us
  transfers between devices with their start and end apart: 28, of which 21 were waited for; matrix products, arithmetic and copies ran while one was open for 11% of the time, Pallas kernels for 0%

profile of v1, /device:TPU:32, one launch (start us, length us, event | category | flops | bytes accessed | tf_op | source)
XLA Modules:
  0.0 323.3 jit_solution(13629001991041114712)
XLA Ops:
  9.8 1.8 constant_dynamic-update-slice_fusion.15
  11.5 1.7 collective-permute-start.9
  13.6 1.2 convert_reduce_fusion
  14.8 1.3 fusion.28
  16.9 2.0 collective-permute-start.10
  19.7 2.6 collective-permute-done.2
  22.4 2.2 collective-permute-start.11
  25.3 5.1 %collective-permute-done.3 = bf16[96,1152]{1,0:T(8,128)(2,1)S(1)} collective-permute-done((bf16[96,1152]{1,0:T(8,128)(2,1)S(1)}, bf16[96,1152]{1,0:T(8,128)(2,1)S(1)}, u32[]{:S(2)}, u32[]{:S(2)}) %collective-permute-start.3) | collective-permute-done | bytes 221216 | tf_op jit(solution)/shard_map/ppermute | solution.py:15
  30.4 1.4 collective-permute-start.4
  32.8 2.3 collective-permute-start.12
  35.9 3.3 %collective-permute-done.4 = bf16[96,1152]{1,0:T(8,128)(2,1)S(1)} collective-permute-done((bf16[96,1152]{1,0:T(8,128)(2,1)S(1)}, bf16[96,1152]{1,0:T(8,128)(2,1)S(1)}, u32[]{:S(2)}, u32[]{:S(2)}) %collective-permute-start.4) | collective-permute-done | bytes 221216 | tf_op jit(solution)/shard_map/ppermute | solution.py:15
  39.1 2.5 collective-permute-start.5
  41.6 1.8 collective-permute-start.13
  44.1 4.9 %collective-permute-done.5 = bf16[96,1152]{1,0:T(8,128)(2,1)S(1)} collective-permute-done((bf16[96,1152]{1,0:T(8,128)(2,1)S(1)}, bf16[96,1152]{1,0:T(8,128)(2,1)S(1)}, u32[]{:S(2)}, u32[]{:S(2)}) %collective-permute-start.5) | collective-permute-done | bytes 221216 | tf_op jit(solution)/shard_map/ppermute | solution.py:15
  49.0 2.0 collective-permute-start.6
  51.0 2.1 collective-permute-start.14
  53.9 3.3 %collective-permute-done.6 = bf16[96,1152]{1,0:T(8,128)(2,1)S(1)} collective-permute-done((bf16[96,1152]{1,0:T(8,128)(2,1)S(1)}, bf16[96,1152]{1,0:T(8,128)(2,1)S(1)}, u32[]{:S(2)}, u32[]{:S(2)}) %collective-permute-start.6) | collective-permute-done | bytes 221216 | tf_op jit(solution)/shard_map/ppermute | solution.py:15
  57.7 2.1 collective-permute-start.15
  60.6 2.5 collective-permute-done.7
  63.8 5.9 %collective-permute-done.8 = bf16[96,1152]{1,0:T(8,128)(2,1)S(1)} collective-permute-done((bf16[96,1152]{1,0:T(8,128)(2,1)S(1)}, bf16[96,1152]{1,0:T(8,128)(2,1)S(1)}, u32[]{:S(2)}, u32[]{:S(2)}) %collective-permute-start.8) | collective-permute-done | bytes 221216 | tf_op jit(solution)/shard_map/ppermute | solution.py:15
  73.9 3.9 %fusion.65 = f32[192,2152]{1,0:T(8,128)S(1)} fusion(bf16[1152,2152]{1,0:T(8,128)(2,1)} %all-gather.3.cloned.1.call-done, bf16[1,192,1152]{2,1,0:T(8,128)(2,1)S(1)} %copy-done, f32[1152]{0:T(1024)S(1)} %copy-done.6, f32[192]{0:T(256)S(1)} %add_rsqrt_fusion, f32[192]{0:T(256)S(1)} %broadcast_multiply_fusion.2), kind=kOutput, calls=%fused_computation.140 | convolution fusion | flops 953081856 | bytes 7059456 | tf_op jit(solution)/shard_map/dot_general | solution.py:85
  77.8 26.3 %all-gather.5.cloned.1.call-done = bf16[2152,1152]{0,1:T(8,128)(2,1)} async-done(((bf16[2152,72]{0,1:T(8,128)(2,1)}), bf16[2152,1152]{0,1:T(8,128)(2,1)}) %all-gather.5.cloned.1.call-update) | async-done | bytes 4958224 | tf_op jit(solution)/shard_map/all_gather | solution.py:87
  104.2 4.1 %convolution_convert_fusion.3 = bf16[192,1152]{1,0:T(8,128)(2,1)S(1)} fusion(bf16[2152,1152]{0,1:T(8,128)(2,1)} %all-gather.5.cloned.1.call-done, f32[192,2152]{1,0:T(8,128)S(1)} %fusion.65), kind=kOutput, calls=%fused_computation.13 | convolution fusion | flops 955915776 | bytes 7053312 | tf_op jit(solution)/shard_map/dot_general | solution.py:88
  108.3 3.7 %collective-permute-start = (bf16[192,1152]{1,0:T(8,128)(2,1)S(1)}, bf16[192,1152]{1,0:T(8,128)(2,1)S(1)}, u32[]{:S(2)}, u32[]{:S(2)}) collective-permute-start(bf16[192,1152]{1,0:T(8,128)(2,1)S(1)} %convolution_convert_fusion.3), channel_id=1, source_target_pairs={{0,1},{1,0},{2,3},{3,2},{4,5},{5,4},{6,7},{7,6},{8,9},{9,8},{10,11... | collective-permute-start | bytes 1327112 | tf_op jit(solution)/shard_map/ppermute | solution.py:20
  113.3 9.2 %collective-permute-done = bf16[192,1152]{1,0:T(8,128)(2,1)S(1)} collective-permute-done((bf16[192,1152]{1,0:T(8,128)(2,1)S(1)}, bf16[192,1152]{1,0:T(8,128)(2,1)S(1)}, u32[]{:S(2)}, u32[]{:S(2)}) %collective-permute-start) | collective-permute-done | bytes 442400 | tf_op jit(solution)/shard_map/ppermute | solution.py:20
  122.8 5.3 %fusion.7 = bf16[192,1152]{1,0:T(8,128)(2,1)S(1)} fusion(bf16[1536,1152]{1,0:T(8,128)(2,1)} %constant_dynamic-update-slice_fusion, s32[1536]{0:T(1024)S(1)} %concatenate.7, s32[192]{0:T(256)S(1)} %iota_add_fusion, bf16[192,1152]{1,0:T(8,128)(2,1)S(1)} %collective-permute-done, bf16[192,1152]{1,0:T(8,128)(2,1)S(1)} %convolution_convert_fusion.3, ...), kind=kOutput, calls=%fused_computation.11 | convolution fusion | flops 1363599360 | bytes 5316096 | tf_op jit(solution)/shard_map/dot_general | solution.py:102
  128.1 3.3 %collective-permute-start.16 = (bf16[192,1152]{1,0:T(8,128)(2,1)S(1)}, bf16[192,1152]{1,0:T(8,128)(2,1)S(1)}, u32[]{:S(2)}, u32[]{:S(2)}) collective-permute-start(bf16[192,1152]{1,0:T(8,128)(2,1)S(1)} %fusion.7), channel_id=1, source_target_pairs={{0,1},{1,0},{2,3},{3,2},{4,5},{5,4},{6,7},{7,6},{8,9},{9,8},{10,11... | collective-permute-start | bytes 1327112 | tf_op jit(solution)/shard_map/ppermute | solution.py:20
  131.5 10.0 %collective-permute-done.16 = bf16[192,1152]{1,0:T(8,128)(2,1)S(1)} collective-permute-done((bf16[192,1152]{1,0:T(8,128)(2,1)S(1)}, bf16[192,1152]{1,0:T(8,128)(2,1)S(1)}, u32[]{:S(2)}, u32[]{:S(2)}) %collective-permute-start.16) | collective-permute-done | bytes 442400 | tf_op jit(solution)/shard_map/ppermute | solution.py:20
  142.2 4.4 %fusion.14 = bf16[192,2152]{1,0:T(8,128)(2,1)S(1)} fusion(f32[192,2152]{1,0:T(8,128)S(1)} %copy-done.2, bf16[2152,1152]{0,1:T(8,128)(2,1)} %all-gather.5.cloned.1.call-done, f32[192,1152]{1,0:T(8,128)S(1)} %subtract_divide_fusion), kind=kOutput, calls=%fused_computation.22 | convolution fusion | flops 960460800 | bytes 8322048 | tf_op jit(solution)/shard_map/rd,fd->rf/dot_general | solution.py:108
  147.5 4.0 %convolution_convert_fusion.1 = bf16[1152,2152]{1,0:T(8,128)(2,1)} fusion(bf16[192,2152]{1,0:T(8,128)(2,1)S(1)} %fusion.14, bf16[1,192,1152]{2,1,0:T(8,128)(2,1)S(1)} %copy-done, f32[1152]{0:T(1024)S(1)} %copy-done.6, f32[192]{0:T(256)S(1)} %add_rsqrt_fusion, f32[192]{0:T(256)S(1)} %broadcast_multiply_fusion.2), kind=kOutput, calls=%fused_computation.1 | convolution fusion | flops 955560960 | bytes 6233088 | tf_op jit(solution)/shard_map/rd,rf->df/dot_general | solution.py:121
  151.8 1.2 copy-done.3
  153.0 3.9 %convolution_convert_fusion = bf16[2152,1152]{0,1:T(8,128)(2,1)} fusion(f32[192,1152]{1,0:T(8,128)S(1)} %subtract_divide_fusion, f32[192,2152]{1,0:T(8,128)S(1)} %copy-done.3), kind=kOutput, calls=%fused_computation | convolution fusion | flops 958394880 | bytes 7495680 | tf_op jit(solution)/shard_map/rf,rd->fd/dot_general | solution.py:128
  158.0 4.0 %convolution_convert_fusion.2 = bf16[192,1152]{1,0:T(8,128)(2,1)S(1)} fusion(bf16[192,2152]{1,0:T(8,128)(2,1)S(1)} %copy-done.5, bf16[1152,2152]{1,0:T(8,128)(2,1)} %all-gather.3.cloned.1.call-done), kind=kOutput, calls=%fused_computation.12 | convolution fusion | flops 952197120 | bytes 6226944 | tf_op jit(solution)/shard_map/rf,df->rd/dot_general | solution.py:111
  162.1 3.1 collective-permute-start.17
  165.1 9.4 %collective-permute-done.17 = bf16[192,1152]{1,0:T(8,128)(2,1)S(1)} collective-permute-done((bf16[192,1152]{1,0:T(8,128)(2,1)S(1)}, bf16[192,1152]{1,0:T(8,128)(2,1)S(1)}, u32[]{:S(2)}, u32[]{:S(2)}) %collective-permute-start.17) | collective-permute-done | bytes 442400 | tf_op jit(solution)/shard_map/ppermute | solution.py:20
  174.9 39.5 %reduce-scatter.7.cloned.1.call-done = bf16[72,2152]{1,0:T(8,128)(2,1)} async-done(((bf16[1152,2152]{1,0:T(8,128)(2,1)}), bf16[72,2152]{1,0:T(8,128)(2,1)}) %reduce-scatter.7.cloned.1.call-update) | async-done | bytes 309904
  214.5 1.4 collective-permute-start.18
  215.9 1.3 fusion.27
  217.2 65.5 %reduce-scatter.9.cloned.1.call-done = bf16[2152,72]{0,1:T(8,128)(2,1)} async-done(((bf16[2152,1152]{0,1:T(8,128)(2,1)}), bf16[2152,72]{0,1:T(8,128)(2,1)}) %reduce-scatter.9.cloned.1.call-update) | async-done | bytes 309904
  282.7 1.5 collective-permute-start.21
  285.2 1.5 collective-permute-start.19
  286.8 4.6 %collective-permute-done.21 = bf16[2152,72]{0,1:T(8,128)(2,1)S(1)} collective-permute-done((bf16[2152,72]{0,1:T(8,128)(2,1)}, bf16[2152,72]{0,1:T(8,128)(2,1)S(1)}, u32[]{:S(2)}, u32[]{:S(2)}) %collective-permute-start.21) | collective-permute-done | bytes 309920 | tf_op jit(solution)/shard_map/ppermute | solution.py:31
  292.4 1.7 collective-permute-start.22
  294.2 2.9 collective-permute-start.20
  297.1 5.7 %collective-permute-done.22 = bf16[2152,72]{0,1:T(8,128)(2,1)S(1)} collective-permute-done((bf16[2152,72]{0,1:T(8,128)(2,1)S(1)}, bf16[2152,72]{0,1:T(8,128)(2,1)S(1)}, u32[]{:S(2)}, u32[]{:S(2)}) %collective-permute-start.22) | collective-permute-done | bytes 309920 | tf_op jit(solution)/shard_map/ppermute | solution.py:31
  302.8 3.0 collective-permute-start.23
  305.9 5.9 %collective-permute-done.20 = bf16[72,2152]{1,0:T(8,128)(2,1)S(1)} collective-permute-done((bf16[72,2152]{1,0:T(8,128)(2,1)S(1)}, bf16[72,2152]{1,0:T(8,128)(2,1)S(1)}, u32[]{:S(2)}, u32[]{:S(2)}) %collective-permute-start.20) | collective-permute-done | bytes 309920 | tf_op jit(solution)/shard_map/ppermute | solution.py:31
  312.6 3.3 %collective-permute-done.23 = bf16[2152,72]{0,1:T(8,128)(2,1)S(1)} collective-permute-done((bf16[2152,72]{0,1:T(8,128)(2,1)S(1)}, bf16[2152,72]{0,1:T(8,128)(2,1)S(1)}, u32[]{:S(2)}, u32[]{:S(2)}) %collective-permute-start.23) | collective-permute-done | bytes 309920 | tf_op jit(solution)/shard_map/ppermute | solution.py:31
  (79 shorter events, 23.8 us)
Async XLA Ops:
  7.2 66.8 %all-gather.3.cloned.1.call-start = ((), (), s32[]{:S(2)}) async-start(), calls=%async_computation.2 | async-start | bytes 5326848 | tf_op jit(solution)/shard_map/all_gather | solution.py:84
  7.9 96.3 %all-gather.5.cloned.1.call-start = ((), (), s32[]{:S(2)}) async-start(), calls=%async_computation.3 | async-start | bytes 5326848 | tf_op jit(solution)/shard_map/all_gather | solution.py:87
  8.6 205.8 %reduce-scatter.7.cloned.1.call-start = ((), (), s32[]{:S(2)}) async-start(), calls=%async_computation.4 | async-start | bytes 5326848
  11.5 5.4 %collective-permute-start.1 = (bf16[96,1152]{1,0:T(8,128)(2,1)S(1)}, bf16[96,1152]{1,0:T(8,128)(2,1)S(1)}, u32[]{:S(2)}, u32[]{:S(2)}) collective-permute-start(bf16[96,1152]{1,0:T(8,128)(2,1)S(1)} %get-tuple-element.6), channel_id=1, source_target_pairs={{30,0},{0,2},{2,4},{4,6},{6,8},{8,10},{10,12},{12,14},{14,16},{16,... | collective-permute-start | bytes 663560 | tf_op jit(solution)/shard_map/ppermute | solution.py:15
  11.5 5.4 %collective-permute-start.9 = (bf16[96,1152]{1,0:T(8,128)(2,1)S(1)}, bf16[96,1152]{1,0:T(8,128)(2,1)S(1)}, u32[]{:S(2)}, u32[]{:S(2)}) collective-permute-start(bf16[96,1152]{1,0:T(8,128)(2,1)S(1)} %get-tuple-element.6), channel_id=1, source_target_pairs={{2,0},{4,2},{6,4},{8,6},{10,8},{12,10},{14,12},{16,14},{18,16},{20... | collective-permute-start | bytes 663560 | tf_op jit(solution)/shard_map/ppermute | solution.py:15
  13.3 60.6 %copy-start = (bf16[1,192,1152]{2,1,0:T(8,128)(2,1)S(1)}, bf16[1,192,1152]{2,1,0:T(8,128)(2,1)}, u32[]{:S(2)}) copy-start(bf16[1,192,1152]{2,1,0:T(8,128)(2,1)} %param.5) | copy-start | bytes 1327108
  13.3 60.6 %copy-start.6 = (f32[1152]{0:T(1024)S(1)}, f32[1152]{0:T(1024)}, u32[]{:S(2)}) copy-start(f32[1152]{0:T(1024)} %param.6) | copy-start | bytes 13828
  16.9 5.4 %collective-permute-start.2 = (bf16[96,1152]{1,0:T(8,128)(2,1)S(1)}, bf16[96,1152]{1,0:T(8,128)(2,1)S(1)}, u32[]{:S(2)}, u32[]{:S(2)}) collective-permute-start(bf16[96,1152]{1,0:T(8,128)(2,1)S(1)} %collective-permute-done.1), channel_id=1, source_target_pairs={{30,0},{0,2},{2,4},{4,6},{6,8},{8,10},{10,12},{12,14},{14,16},{16,... | collective-permute-start | bytes 663560 | tf_op jit(solution)/shard_map/ppermute | solution.py:15
  16.9 5.5 %collective-permute-start.10 = (bf16[96,1152]{1,0:T(8,128)(2,1)S(1)}, bf16[96,1152]{1,0:T(8,128)(2,1)S(1)}, u32[]{:S(2)}, u32[]{:S(2)}) collective-permute-start(bf16[96,1152]{1,0:T(8,128)(2,1)S(1)} %collective-permute-done.9), channel_id=1, source_target_pairs={{2,0},{4,2},{6,4},{8,6},{10,8},{12,10},{14,12},{16,14},{18,16},{20... | collective-permute-start | bytes 663560 | tf_op jit(solution)/shard_map/ppermute | solution.py:15
  22.3 8.1 %collective-permute-start.3 = (bf16[96,1152]{1,0:T(8,128)(2,1)S(1)}, bf16[96,1152]{1,0:T(8,128)(2,1)S(1)}, u32[]{:S(2)}, u32[]{:S(2)}) collective-permute-start(bf16[96,1152]{1,0:T(8,128)(2,1)S(1)} %collective-permute-done.2), channel_id=1, source_target_pairs={{30,0},{0,2},{2,4},{4,6},{6,8},{8,10},{10,12},{12,14},{14,16},{16,... | collective-permute-start | bytes 663560 | tf_op jit(solution)/shard_map/ppermute | solution.py:15
  22.4 10.4 %collective-permute-start.11 = (bf16[96,1152]{1,0:T(8,128)(2,1)S(1)}, bf16[96,1152]{1,0:T(8,128)(2,1)S(1)}, u32[]{:S(2)}, u32[]{:S(2)}) collective-permute-start(bf16[96,1152]{1,0:T(8,128)(2,1)S(1)} %collective-permute-done.10), channel_id=1, source_target_pairs={{2,0},{4,2},{6,4},{8,6},{10,8},{12,10},{14,12},{16,14},{18,16},{20... | collective-permute-start | bytes 663560 | tf_op jit(solution)/shard_map/ppermute | solution.py:15
  30.4 8.7 %collective-permute-start.4 = (bf16[96,1152]{1,0:T(8,128)(2,1)S(1)}, bf16[96,1152]{1,0:T(8,128)(2,1)S(1)}, u32[]{:S(2)}, u32[]{:S(2)}) collective-permute-start(bf16[96,1152]{1,0:T(8,128)(2,1)S(1)} %collective-permute-done.3), channel_id=1, source_target_pairs={{30,0},{0,2},{2,4},{4,6},{6,8},{8,10},{10,12},{12,14},{14,16},{16,... | collective-permute-start | bytes 663560 | tf_op jit(solution)/shard_map/ppermute | solution.py:15
  32.8 8.8 %collective-permute-start.12 = (bf16[96,1152]{1,0:T(8,128)(2,1)S(1)}, bf16[96,1152]{1,0:T(8,128)(2,1)S(1)}, u32[]{:S(2)}, u32[]{:S(2)}) collective-permute-start(bf16[96,1152]{1,0:T(8,128)(2,1)S(1)} %collective-permute-done.11), channel_id=1, source_target_pairs={{2,0},{4,2},{6,4},{8,6},{10,8},{12,10},{14,12},{16,14},{18,16},{20... | collective-permute-start | bytes 663560 | tf_op jit(solution)/shard_map/ppermute | solution.py:15
  39.1 9.8 %collective-permute-start.5 = (bf16[96,1152]{1,0:T(8,128)(2,1)S(1)}, bf16[96,1152]{1,0:T(8,128)(2,1)S(1)}, u32[]{:S(2)}, u32[]{:S(2)}) collective-permute-start(bf16[96,1152]{1,0:T(8,128)(2,1)S(1)} %collective-permute-done.4), channel_id=1, source_target_pairs={{30,0},{0,2},{2,4},{4,6},{6,8},{8,10},{10,12},{12,14},{14,16},{16,... | collective-permute-start | bytes 663560 | tf_op jit(solution)/shard_map/ppermute | solution.py:15
  41.6 9.4 %collective-permute-start.13 = (bf16[96,1152]{1,0:T(8,128)(2,1)S(1)}, bf16[96,1152]{1,0:T(8,128)(2,1)S(1)}, u32[]{:S(2)}, u32[]{:S(2)}) collective-permute-start(bf16[96,1152]{1,0:T(8,128)(2,1)S(1)} %collective-permute-done.12), channel_id=1, source_target_pairs={{2,0},{4,2},{6,4},{8,6},{10,8},{12,10},{14,12},{16,14},{18,16},{20... | collective-permute-start | bytes 663560 | tf_op jit(solution)/shard_map/ppermute | solution.py:15
  49.0 8.2 %collective-permute-start.6 = (bf16[96,1152]{1,0:T(8,128)(2,1)S(1)}, bf16[96,1152]{1,0:T(8,128)(2,1)S(1)}, u32[]{:S(2)}, u32[]{:S(2)}) collective-permute-start(bf16[96,1152]{1,0:T(8,128)(2,1)S(1)} %collective-permute-done.5), channel_id=1, source_target_pairs={{30,0},{0,2},{2,4},{4,6},{6,8},{8,10},{10,12},{12,14},{14,16},{16,... | collective-permute-start | bytes 663560 | tf_op jit(solution)/shard_map/ppermute | solution.py:15
  51.0 6.7 %collective-permute-start.14 = (bf16[96,1152]{1,0:T(8,128)(2,1)S(1)}, bf16[96,1152]{1,0:T(8,128)(2,1)S(1)}, u32[]{:S(2)}, u32[]{:S(2)}) collective-permute-start(bf16[96,1152]{1,0:T(8,128)(2,1)S(1)} %collective-permute-done.13), channel_id=1, source_target_pairs={{2,0},{4,2},{6,4},{8,6},{10,8},{12,10},{14,12},{16,14},{18,16},{20... | collective-permute-start | bytes 663560 | tf_op jit(solution)/shard_map/ppermute | solution.py:15
  57.1 6.0 %collective-permute-start.7 = (bf16[96,1152]{1,0:T(8,128)(2,1)S(1)}, bf16[96,1152]{1,0:T(8,128)(2,1)S(1)}, u32[]{:S(2)}, u32[]{:S(2)}) collective-permute-start(bf16[96,1152]{1,0:T(8,128)(2,1)S(1)} %collective-permute-done.6), channel_id=1, source_target_pairs={{30,0},{0,2},{2,4},{4,6},{6,8},{8,10},{10,12},{12,14},{14,16},{16,... | collective-permute-start | bytes 663560 | tf_op jit(solution)/shard_map/ppermute | solution.py:15
  57.7 54.9 %collective-permute-start.15 = (bf16[96,1152]{1,0:T(8,128)(2,1)S(1)}, bf16[96,1152]{1,0:T(8,128)(2,1)S(1)}, u32[]{:S(2)}, u32[]{:S(2)}) collective-permute-start(bf16[96,1152]{1,0:T(8,128)(2,1)S(1)} %collective-permute-done.14), channel_id=1, source_target_pairs={{2,0},{4,2},{6,4},{8,6},{10,8},{12,10},{14,12},{16,14},{18,16},{20... | collective-permute-start | bytes 663560 | tf_op jit(solution)/shard_map/ppermute | solution.py:15
  63.1 6.6 %collective-permute-start.8 = (bf16[96,1152]{1,0:T(8,128)(2,1)S(1)}, bf16[96,1152]{1,0:T(8,128)(2,1)S(1)}, u32[]{:S(2)}, u32[]{:S(2)}) collective-permute-start(bf16[96,1152]{1,0:T(8,128)(2,1)S(1)} %collective-permute-done.7), channel_id=1, source_target_pairs={{30,0},{0,2},{2,4},{4,6},{6,8},{8,10},{10,12},{12,14},{14,16},{16,... | collective-permute-start | bytes 663560 | tf_op jit(solution)/shard_map/ppermute | solution.py:15
  77.8 26.3 %copy-start.1 = (f32[192,2152]{1,0:T(8,128)}, f32[192,2152]{1,0:T(8,128)S(1)}, u32[]{:S(2)}) copy-start(f32[192,2152]{1,0:T(8,128)S(1)} %fusion.65) | copy-start | bytes 4958212
  108.3 14.2 %collective-permute-start = (bf16[192,1152]{1,0:T(8,128)(2,1)S(1)}, bf16[192,1152]{1,0:T(8,128)(2,1)S(1)}, u32[]{:S(2)}, u32[]{:S(2)}) collective-permute-start(bf16[192,1152]{1,0:T(8,128)(2,1)S(1)} %convolution_convert_fusion.3), channel_id=1, source_target_pairs={{0,1},{1,0},{2,3},{3,2},{4,5},{5,4},{6,7},{7,6},{8,9},{9,8},{10,11... | collective-permute-start | bytes 1327112 | tf_op jit(solution)/shard_map/ppermute | solution.py:20
  128.1 14.1 %copy-start.2 = (f32[192,2152]{1,0:T(8,128)S(1)}, f32[192,2152]{1,0:T(8,128)}, u32[]{:S(2)}) copy-start(f32[192,2152]{1,0:T(8,128)} %copy-done.1) | copy-start | bytes 4958212
  128.1 13.3 %collective-permute-start.16 = (bf16[192,1152]{1,0:T(8,128)(2,1)S(1)}, bf16[192,1152]{1,0:T(8,128)(2,1)S(1)}, u32[]{:S(2)}, u32[]{:S(2)}) collective-permute-start(bf16[192,1152]{1,0:T(8,128)(2,1)S(1)} %fusion.7), channel_id=1, source_target_pairs={{0,1},{1,0},{2,3},{3,2},{4,5},{5,4},{6,7},{7,6},{8,9},{9,8},{10,11... | collective-permute-start | bytes 1327112 | tf_op jit(solution)/shard_map/ppermute | solution.py:20
  146.6 0.9 copy-start.4
  151.5 1.4 copy-start.3
  151.6 131.1 %reduce-scatter.9.cloned.1.call-start = ((), (), s32[]{:S(2)}) async-start(), calls=%async_computation.5 | async-start | bytes 5326848
  156.9 1.1 copy-start.5
  162.1 12.5 %collective-permute-start.17 = (bf16[192,1152]{1,0:T(8,128)(2,1)S(1)}, bf16[192,1152]{1,0:T(8,128)(2,1)S(1)}, u32[]{:S(2)}, u32[]{:S(2)}) collective-permute-start(bf16[192,1152]{1,0:T(8,128)(2,1)S(1)} %convolution_convert_fusion.2), channel_id=1, source_target_pairs={{0,1},{1,0},{2,3},{3,2},{4,5},{5,4},{6,7},{7,6},{8,9},{9,8},{10,11... | collective-permute-start | bytes 1327112 | tf_op jit(solution)/shard_map/ppermute | solution.py:20
  214.5 69.7 %collective-permute-start.18 = (bf16[72,2152]{1,0:T(8,128)(2,1)}, bf16[72,2152]{1,0:T(8,128)(2,1)S(1)}, u32[]{:S(2)}, u32[]{:S(2)}) collective-permute-start(bf16[72,2152]{1,0:T(8,128)(2,1)} %reduce-scatter.7.cloned.1.call-done), channel_id=1, source_target_pairs={{0,32},{32,0},{64,96},{96,64},{128,160},{160,128},{192,224},{224,1... | collective-permute-start | bytes 929672 | tf_op jit(solution)/shard_map/ppermute | solution.py:31
  282.7 8.6 %collective-permute-start.21 = (bf16[2152,72]{0,1:T(8,128)(2,1)}, bf16[2152,72]{0,1:T(8,128)(2,1)S(1)}, u32[]{:S(2)}, u32[]{:S(2)}) collective-permute-start(bf16[2152,72]{0,1:T(8,128)(2,1)} %reduce-scatter.9.cloned.1.call-done), channel_id=1, source_target_pairs={{0,32},{32,0},{64,96},{96,64},{128,160},{160,128},{192,224},{224,1... | collective-permute-start | bytes 929672 | tf_op jit(solution)/shard_map/ppermute | solution.py:31
  285.2 8.9 %collective-permute-start.19 = (bf16[72,2152]{1,0:T(8,128)(2,1)S(1)}, bf16[72,2152]{1,0:T(8,128)(2,1)S(1)}, u32[]{:S(2)}, u32[]{:S(2)}) collective-permute-start(bf16[72,2152]{1,0:T(8,128)(2,1)S(1)} %add_convert_fusion.3), channel_id=1, source_target_pairs={{0,64},{32,96},{64,0},{96,32},{128,192},{160,224},{192,128},{224,1... | collective-permute-start | bytes 929672 | tf_op jit(solution)/shard_map/ppermute | solution.py:31
  292.4 10.4 %collective-permute-start.22 = (bf16[2152,72]{0,1:T(8,128)(2,1)S(1)}, bf16[2152,72]{0,1:T(8,128)(2,1)S(1)}, u32[]{:S(2)}, u32[]{:S(2)}) collective-permute-start(bf16[2152,72]{0,1:T(8,128)(2,1)S(1)} %add_convert_fusion.1), channel_id=1, source_target_pairs={{0,64},{32,96},{64,0},{96,32},{128,192},{160,224},{192,128},{224,1... | collective-permute-start | bytes 929672 | tf_op jit(solution)/shard_map/ppermute | solution.py:31
  294.2 17.6 %collective-permute-start.20 = (bf16[72,2152]{1,0:T(8,128)(2,1)S(1)}, bf16[72,2152]{1,0:T(8,128)(2,1)S(1)}, u32[]{:S(2)}, u32[]{:S(2)}) collective-permute-start(bf16[72,2152]{1,0:T(8,128)(2,1)S(1)} %add_convert_fusion.2), channel_id=1, source_target_pairs={{0,128},{32,160},{64,192},{96,224},{128,0},{160,32},{192,64},{224,... | collective-permute-start | bytes 929672 | tf_op jit(solution)/shard_map/ppermute | solution.py:31
  302.8 13.1 %collective-permute-start.23 = (bf16[2152,72]{0,1:T(8,128)(2,1)S(1)}, bf16[2152,72]{0,1:T(8,128)(2,1)S(1)}, u32[]{:S(2)}, u32[]{:S(2)}) collective-permute-start(bf16[2152,72]{0,1:T(8,128)(2,1)S(1)} %add_convert_fusion), channel_id=1, source_target_pairs={{0,128},{32,160},{64,192},{96,224},{128,0},{160,32},{192,64},{224,... | collective-permute-start | bytes 929672 | tf_op jit(solution)/shard_map/ppermute | solution.py:31
Sparse Core Ops, SparseCore 0:
  9.8 49.5 all-gather.2
  61.2 42.8 all-gather.4
  151.7 62.7 reduce-scatter.6
  216.9 65.7 reduce-scatter.8

commit v2 on v1

v2 whole, which is shorter than its diff:
```python
import jax
import jax.numpy as jnp
from jax import lax
from jax.sharding import Mesh
from jax.sharding import PartitionSpec as P

ln_eps = 1e-06
norm_eps = 1e-06
logit_scale = 10.0
logit_bias = -2.0


def passed_along(block, axis, distance):
    devices = range(lax.axis_size(axis))
    route = [((i - distance) % len(devices), i) for i in devices]
    return lax.ppermute(block, axis, route)


def core_swap(block):
    return lax.ppermute(block, "core", [(0, 1), (1, 0)])


def swapped_sum(partial, axis):
    mine = partial.astype(jnp.bfloat16)
    other = lax.ppermute(mine, axis, [(0, 1), (1, 0)])
    return mine.astype(jnp.float32) + other.astype(jnp.float32)


def doubling_sum(parts, axis):
    size = lax.axis_size(axis)
    mine = [p.astype(jnp.bfloat16) for p in parts]
    totals = None
    bit = 1
    while bit < size:
        route = [(i, i ^ bit) for i in range(size)]
        others = [lax.ppermute(m, axis, route) for m in mine]
        totals = [m.astype(jnp.float32) + o.astype(jnp.float32) for m, o in zip(mine, others)]
        mine = [t.astype(jnp.bfloat16) for t in totals]
        bit *= 2
    return totals


def parity_split(values, core, chips):
    lead = values.shape[:-1]
    blocks = values.reshape(lead + (chips, 2, values.shape[-1] // (2 * chips)))
    axis = blocks.ndim - 2
    own = lax.dynamic_index_in_dim(blocks, core, axis=axis, keepdims=False)
    other = lax.dynamic_index_in_dim(blocks, 1 - core, axis=axis, keepdims=False)
    half = lead + (values.shape[-1] // 2,)
    return own.reshape(half), other.reshape(half)


def parity_join(own, other, core, chips):
    lead = own.shape[:-1]
    shape = lead + (chips, 1, own.shape[-1] // chips)
    own = own.reshape(shape)
    other = other.reshape(shape)
    even = jnp.where(core == 0, own, other)
    odd = jnp.where(core == 0, other, own)
    return jnp.concatenate([even, odd], axis=-2).reshape(lead + (2 * own.shape[-1] * chips,))


def gelu_tanh(values):
    return jax.nn.gelu(values, approximate=True)


def unit_rows(values):
    return values / jnp.sqrt(jnp.sum(values * values, axis=-1, keepdims=True) + norm_eps)


def body(pooled, ln_gain, w_in, w_out, texts):
    rows = pooled[0].astype(jnp.float32)
    images = rows.shape[0]
    chip = lax.axis_index("z")
    chips = lax.axis_size("z")
    core = lax.axis_index("core")
    block_index = chip * 2 + core

    text_b = unit_rows(texts[0].astype(jnp.float32)).astype(jnp.bfloat16)
    block_rows = text_b.shape[0]
    offset = lax.axis_index("tensor") * block_rows
    pair = jnp.concatenate([text_b, core_swap(text_b)], axis=0)
    within = jnp.arange(block_rows, dtype=jnp.int32)

    def pair_columns(source_chip):
        first = (source_chip * 2 + core) * images + offset + within
        second = (source_chip * 2 + 1 - core) * images + offset + within
        return jnp.concatenate([first, second])

    blocks = [pair]
    sources = [chip]
    ahead = pair
    for step in range(1, chips // 2 + 1):
        ahead = passed_along(ahead, "z", 1)
        blocks.append(ahead)
        sources.append((chip - step) % chips)
    behind = pair
    for step in range(1, (chips - 1) // 2 + 1):
        behind = passed_along(behind, "z", -1)
        blocks.append(behind)
        sources.append((chip + step) % chips)
    all_texts = jnp.concatenate(blocks, axis=0)
    columns = jnp.concatenate([pair_columns(s) for s in sources], axis=0)

    own_in = lax.all_gather(w_in, "z", axis=0, tiled=True)
    other_in = core_swap(own_in)
    own_out = lax.all_gather(w_out, "z", axis=1, tiled=True)
    other_out = core_swap(own_out)

    row_mean = jnp.mean(rows, axis=1, keepdims=True)
    centred = rows - row_mean
    inv_std = lax.rsqrt(jnp.mean(centred * centred, axis=1, keepdims=True) + ln_eps)
    normal_rows = centred * inv_std
    unit_in = (normal_rows * ln_gain).astype(jnp.bfloat16)
    unit_own, unit_other = parity_split(unit_in, core, chips)
    pre_act = jnp.dot(unit_own, own_in, preferred_element_type=jnp.float32) + jnp.dot(
        unit_other, other_in, preferred_element_type=jnp.float32
    )
    hidden = gelu_tanh(pre_act).astype(jnp.bfloat16)
    mix_parts = jnp.concatenate(
        [
            jnp.dot(hidden, own_out, preferred_element_type=jnp.float32),
            jnp.dot(hidden, other_out, preferred_element_type=jnp.float32),
        ],
        axis=1,
    )
    mix_sum = swapped_sum(mix_parts, "tensor")
    half = mix_sum.shape[1] // 2
    mixed = rows + parity_join(mix_sum[:, :half], mix_sum[:, half:], core, chips)
    row_norm = jnp.sqrt(jnp.sum(mixed * mixed, axis=1, keepdims=True) + norm_eps)
    image_unit = mixed / row_norm
    image_b = image_unit.astype(jnp.bfloat16)
    image_places = block_index * images + jnp.arange(images, dtype=jnp.int32)

    logits = (
        logit_scale
        * jnp.einsum("rd,cd->rc", image_b, all_texts, preferred_element_type=jnp.float32)
        + logit_bias
    )
    match = (image_places[:, None] == columns[None, :]).astype(jnp.float32)
    weights = (jax.nn.sigmoid(logits) - match).astype(jnp.bfloat16)
    running = jnp.dot(weights, all_texts, preferred_element_type=jnp.float32)
    grad_unit = swapped_sum(logit_scale * running, "tensor")
    grad_mixed = (
        grad_unit - image_unit * jnp.sum(image_unit * grad_unit, axis=1, keepdims=True)
    ) / row_norm
    grad_b = grad_mixed.astype(jnp.bfloat16)
    grad_own, grad_other = parity_split(grad_b, core, chips)
    grad_hidden = jnp.einsum(
        "rd,fd->rf", grad_own, own_out, preferred_element_type=jnp.float32
    ) + jnp.einsum("rd,fd->rf", grad_other, other_out, preferred_element_type=jnp.float32)
    _, gelu_back = jax.vjp(gelu_tanh, pre_act)
    grad_pre = gelu_back(grad_hidden)[0].astype(jnp.bfloat16)
    unit_parts = jnp.concatenate(
        [
            jnp.einsum("rf,df->rd", grad_pre, own_in, preferred_element_type=jnp.float32),
            jnp.einsum("rf,df->rd", grad_pre, other_in, preferred_element_type=jnp.float32),
        ],
        axis=1,
    )
    unit_sum = swapped_sum(unit_parts, "tensor")
    grad_unit_in = parity_join(unit_sum[:, :half], unit_sum[:, half:], core, chips)
    scaled = grad_unit_in * ln_gain
    grad_rows = inv_std * (
        scaled
        - jnp.mean(scaled, axis=1, keepdims=True)
        - normal_rows * jnp.mean(scaled * normal_rows, axis=1, keepdims=True)
    )
    grad_pooled = (grad_mixed + grad_rows)[None]

    out_own = jnp.einsum("rf,rd->fd", hidden, grad_own, preferred_element_type=jnp.float32)
    out_other = jnp.einsum("rf,rd->fd", hidden, grad_other, preferred_element_type=jnp.float32)
    out_chip = out_own.astype(jnp.bfloat16).astype(jnp.float32) + core_swap(
        out_other.astype(jnp.bfloat16)
    ).astype(jnp.float32)
    grad_out_part = lax.psum_scatter(
        out_chip.astype(jnp.bfloat16), "z", scatter_dimension=1, tiled=True
    )
    in_own = jnp.einsum("rd,rf->df", unit_own, grad_pre, preferred_element_type=jnp.float32)
    in_other = jnp.einsum("rd,rf->df", unit_other, grad_pre, preferred_element_type=jnp.float32)
    in_chip = in_own.astype(jnp.bfloat16).astype(jnp.float32) + core_swap(
        in_other.astype(jnp.bfloat16)
    ).astype(jnp.float32)
    grad_in_part = lax.psum_scatter(
        in_chip.astype(jnp.bfloat16), "z", scatter_dimension=0, tiled=True
    )
    grad_in, grad_out = doubling_sum([grad_in_part, grad_out_part], "dp")
    return (grad_pooled, grad_in, grad_out)


def solution(mesh):
    fsdp = mesh.shape["fsdp"]
    chip_mesh = Mesh(
        mesh.devices.reshape(mesh.shape["dp"], fsdp // 2, 2, mesh.shape["tensor"]),
        ("dp", "z", "core", "tensor"),
    )
    placed = (
        P("dp", ("z", "core"), None),
        P(),
        P(("z", "core"), "tensor"),
        P("tensor", ("z", "core")),
        P("dp", ("z", "core", "tensor"), None),
    )
    return jax.shard_map(
        body,
        mesh=chip_mesh,
        in_specs=placed,
        out_specs=(
            P("dp", ("z", "core"), None),
            P(("z", "core"), "tensor"),
            P("tensor", ("z", "core")),
        ),
        check_vma=False,
    )
```

time: 326 us -> 312 us (0.957)
  waiting for transfers between devices: 211 us -> 196 us
  starting transfers between devices: 42.8 us -> 30 us
  local copies, waits for them, and re-layouts: 13.9 us -> 23.8 us
  other arithmetic: 12.2 us -> 18.1 us
    unnamed x6, waiting for transfers between devices: 106 us -> 46.7 us
    all_gather x2, waiting for transfers between devices: 26.3 us -> 75.9 us  [the longest x1 41.1 us: body(): own_in = lax.all_gather(w_in, 'z', axis=0, tiled=True)]
    ppermute x15 -> x7, starting transfers between devices: 20.3 us -> 8.02 us  [passed_along(): return lax.ppermute(block, axis, route)]
    ppermute x15 -> x7, waiting for transfers between devices: 30.1 us -> 17.9 us  [passed_along(): return lax.ppermute(block, axis, route)]
    ppermute x0 -> x5, waiting for transfers between devices: none -> 9.34 us  [core_swap(): return lax.ppermute(block, 'core', [(0, 1), (1, 0)])]
    select_n x0 -> x4, local copies, waits for them, and re-layouts: none -> 3.53 us  [the longest x2 2.28 us: parity_join(): even = jnp.where(core == 0, own, other)]
    unnamed x28 -> x49, local copies, waits for them, and re-layouts: 13.1 us -> 11.9 us
    dot_general x6 -> x12, matrix products: 24.3 us -> 23.9 us  [the longest x1 4.32 us: body(): jnp.dot(unit_other, other_in, preferred_element_type=jnp.float32)]
  transfers between devices with their start and end apart: 28 -> 25, of which waited for: 21 -> 17; matrix products, arithmetic and copies ran while one was open for 11% -> 18% of each run, Pallas kernels for 0% -> 0%
where the time goes in v2:
time: 312 us; the launch traced here: 311 us
  waiting for transfers between devices  196 us (63%)
  starting transfers between devices  30 us (10%)
  matrix products  29.2 us (9%)
  local copies, waits for them, and re-layouts  23.8 us (8%)
  other arithmetic  18.1 us (6%)
  between operations  14.3 us (5%)
    unnamed x6, waiting for transfers between devices  46.7 us
    all_gather x1, waiting for transfers between devices, body(): own_in = lax.all_gather(w_in, 'z', axis=0, tiled=True)  41.1 us
    all_gather x1, waiting for transfers between devices, body(): own_out = lax.all_gather(w_out, 'z', axis=1, tiled=True)  34.8 us
    ppermute x3, waiting for transfers between devices, swapped_sum(): other = lax.ppermute(mine, axis, [(0, 1), (1, 0)])  27.9 us
    ppermute x6, waiting for transfers between devices, doubling_sum(): others = [lax.ppermute(m, axis, route) for m in mine]  18.1 us
    ppermute x7, waiting for transfers between devices, passed_along(): return lax.ppermute(block, axis, route)  17.9 us
    ppermute x6, starting transfers between devices, doubling_sum(): others = [lax.ppermute(m, axis, route) for m in mine]  12.2 us
    unnamed x49, local copies, waits for them, and re-layouts  11.9 us
  transfers between devices with their start and end apart: 25, of which 17 were waited for; matrix products, arithmetic and copies ran while one was open for 18% of the time, Pallas kernels for 0%

profile of v2, /device:TPU:32, one launch (start us, length us, event | category | flops | bytes accessed | tf_op | source)
XLA Modules:
  0.0 311.2 jit_solution(2663169426499096593)
XLA Ops:
  9.8 1.8 constant_dynamic-update-slice_fusion.8
  14.3 1.9 collective-permute-start.4
  16.5 41.1 %all-gather.3.cloned.1.call-done = bf16[576,2152]{1,0:T(8,128)(2,1)} async-done(((bf16[72,2152]{1,0:T(8,128)(2,1)}), bf16[576,2152]{1,0:T(8,128)(2,1)}) %all-gather.3.cloned.1.call-update) | async-done | bytes 2479120 | tf_op jit(solution)/shard_map/all_gather | solution.py:105
  58.0 1.7 collective-permute-start.5
  61.1 9.4 %collective-permute-done.8 = bf16[192,1152]{1,0:T(8,128)(2,1)} collective-permute-done((bf16[192,1152]{1,0:T(8,128)(2,1)}, bf16[192,1152]{1,0:T(8,128)(2,1)}, u32[]{:S(2)}, u32[]{:S(2)}) %collective-permute-start.8) | collective-permute-done | bytes 442400 | tf_op jit(solution)/shard_map/ppermute | solution.py:16
  70.5 2.0 collective-permute-start.9
  72.9 34.8 %all-gather.5.cloned.1.call-done = bf16[2152,576]{0,1:T(8,128)(2,1)} async-done(((bf16[2152,72]{0,1:T(8,128)(2,1)}), bf16[2152,576]{0,1:T(8,128)(2,1)}) %all-gather.5.cloned.1.call-update) | async-done | bytes 2479120 | tf_op jit(solution)/shard_map/all_gather | solution.py:107
  107.7 1.7 constant_dynamic-update-slice_fusion.7
  109.4 1.9 constant_dynamic-update-slice_fusion.6
  113.3 1.8 constant_dynamic-update-slice_fusion.5
  115.1 1.8 constant_dynamic-update-slice_fusion.4
  116.9 8.0 %collective-permute-done.7 = bf16[192,1152]{1,0:T(8,128)(2,1)S(1)} collective-permute-done((bf16[192,1152]{1,0:T(8,128)(2,1)}, bf16[192,1152]{1,0:T(8,128)(2,1)S(1)}, u32[]{:S(2)}, u32[]{:S(2)}) %collective-permute-start.7) | collective-permute-done | bytes 442400 | tf_op jit(solution)/shard_map/ppermute | solution.py:16
  125.7 1.8 constant_dynamic-update-slice_fusion.2
  128.5 4.3 %multiply_convert_fusion = (bf16[192,2152]{1,0:T(8,128)(2,1)S(1)}, f32[192,2152]{1,0:T(8,128)}) fusion(f32[192,2152]{1,0:T(8,128)S(1)} %fusion.45, bf16[192,576]{0,1:T(8,128)(2,1)S(1)} %bitcast.88, bf16[576,2152]{1,0:T(8,128)(2,1)} %collective-permute-done), kind=kOutput, calls=%fused_computation.27 | convolution fusion | flops 480119808 | bytes 6832128 | tf_op jit(solution)/shard_map/dot_general | solution.py:116
  135.1 3.1 collective-permute-start.2
  138.2 1.8 constant_dynamic-update-slice_fusion.1
  140.8 7.6 %collective-permute-done.2 = bf16[192,1152]{1,0:T(8,128)(2,1)S(1)} collective-permute-done((bf16[192,1152]{1,0:T(8,128)(2,1)S(1)}, bf16[192,1152]{1,0:T(8,128)(2,1)S(1)}, u32[]{:S(2)}, u32[]{:S(2)}) %collective-permute-start.2) | collective-permute-done | bytes 442400 | tf_op jit(solution)/shard_map/ppermute | solution.py:25
  150.4 5.3 %fusion.7 = bf16[192,1152]{1,0:T(8,128)(2,1)S(1)} fusion(bf16[1536,1152]{1,0:T(8,128)(2,1)} %constant_dynamic-update-slice_fusion, s32[1536]{0:T(1024)S(1)} %copy-done.17, s32[192]{0:T(256)S(1)} %copy-done.20, f32[192,1152]{1,0:T(8,128)S(1)} %copy.31, bf16[1,192,1152]{2,1,0:T(8,128)(2,1)S(1)} %copy-done, f32[192]{0:T(256)S(1)} %add_sqrt_fusion), kind=kOutput, calls=%fused_computation.17 | convolution fusion | flops 1362935808 | bytes 5316096 | tf_op jit(solution)/shard_map/dot_general | solution.py:142
  155.8 3.0 collective-permute-start.11
  158.8 9.4 %collective-permute-done.11 = bf16[192,1152]{1,0:T(8,128)(2,1)S(1)} collective-permute-done((bf16[192,1152]{1,0:T(8,128)(2,1)S(1)}, bf16[192,1152]{1,0:T(8,128)(2,1)S(1)}, u32[]{:S(2)}, u32[]{:S(2)}) %collective-permute-start.11) | collective-permute-done | bytes 442400 | tf_op jit(solution)/shard_map/ppermute | solution.py:25
  169.6 2.1 copy.34
  173.7 4.7 %collective-permute-done.17 = bf16[2152,576]{0,1:T(8,128)(2,1)S(1)} collective-permute-done((bf16[2152,576]{0,1:T(8,128)(2,1)S(1)}, bf16[2152,576]{0,1:T(8,128)(2,1)S(1)}, u32[]{:S(2)}, u32[]{:S(2)}) %collective-permute-start.17) | collective-permute-done | bytes 2479136 | tf_op jit(solution)/shard_map/ppermute | solution.py:20
  178.5 2.4 add_convert_fusion
  181.2 2.7 fusion.46
  184.2 1.8 fusion.14
  187.1 4.6 %collective-permute-done.13 = bf16[576,2152]{1,0:T(8,128)(2,1)S(1)} collective-permute-done((bf16[576,2152]{1,0:T(8,128)(2,1)S(1)}, bf16[576,2152]{1,0:T(8,128)(2,1)S(1)}, u32[]{:S(2)}, u32[]{:S(2)}) %collective-permute-start.13) | collective-permute-done | bytes 2479136 | tf_op jit(solution)/shard_map/ppermute | solution.py:20
  191.7 2.5 add_convert_fusion.1
  194.2 2.7 convolution_convert_fusion.5
  196.9 2.7 convolution_convert_fusion.4
  199.8 2.9 collective-permute-start.12
  202.7 10.9 %collective-permute-done.12 = bf16[192,1152]{1,0:T(8,128)(2,1)S(1)} collective-permute-done((bf16[192,1152]{1,0:T(8,128)(2,1)S(1)}, bf16[192,1152]{1,0:T(8,128)(2,1)S(1)}, u32[]{:S(2)}, u32[]{:S(2)}) %collective-permute-start.12) | collective-permute-done | bytes 442400 | tf_op jit(solution)/shard_map/ppermute | solution.py:25
  214.8 2.1 copy.35
  217.9 1.5 multiply_reduce_fusion
  221.9 1.5 fusion.27
  223.4 2.5 reduce-scatter.9.cloned.1.call-done
  226.0 1.3 collective-permute-start.18
  227.3 2.6 fusion.22
  229.9 42.7 %reduce-scatter.7.cloned.1.call-done = bf16[72,2152]{1,0:T(8,128)(2,1)} async-done(((bf16[576,2152]{1,0:T(8,128)(2,1)}), bf16[72,2152]{1,0:T(8,128)(2,1)}) %reduce-scatter.7.cloned.1.call-update) | async-done | bytes 309904
  272.6 1.5 collective-permute-start.14
  274.2 1.5 collective-permute-start.19
  275.7 4.0 %collective-permute-done.14 = bf16[72,2152]{1,0:T(8,128)(2,1)S(1)} collective-permute-done((bf16[72,2152]{1,0:T(8,128)(2,1)}, bf16[72,2152]{1,0:T(8,128)(2,1)S(1)}, u32[]{:S(2)}, u32[]{:S(2)}) %collective-permute-start.14) | collective-permute-done | bytes 309920 | tf_op jit(solution)/shard_map/ppermute | solution.py:36
  280.8 1.6 collective-permute-start.15
  282.4 1.8 collective-permute-done.19
  284.3 3.2 %collective-permute-start.20 = (bf16[2152,72]{0,1:T(8,128)(2,1)S(1)}, bf16[2152,72]{0,1:T(8,128)(2,1)S(1)}, u32[]{:S(2)}, u32[]{:S(2)}) collective-permute-start(bf16[2152,72]{0,1:T(8,128)(2,1)S(1)} %add_convert_fusion.2), channel_id=1, source_target_pairs={{0,128},{32,160},{64,192},{96,224},{128,0},{160,32},{192,64},{224,... | collective-permute-start | bytes 929672 | tf_op jit(solution)/shard_map/ppermute | solution.py:36
  287.5 3.7 %collective-permute-done.15 = bf16[72,2152]{1,0:T(8,128)(2,1)S(1)} collective-permute-done((bf16[72,2152]{1,0:T(8,128)(2,1)S(1)}, bf16[72,2152]{1,0:T(8,128)(2,1)S(1)}, u32[]{:S(2)}, u32[]{:S(2)}) %collective-permute-start.15) | collective-permute-done | bytes 309920 | tf_op jit(solution)/shard_map/ppermute | solution.py:36
  291.3 3.1 %collective-permute-start.16 = (bf16[72,2152]{1,0:T(8,128)(2,1)S(1)}, bf16[72,2152]{1,0:T(8,128)(2,1)S(1)}, u32[]{:S(2)}, u32[]{:S(2)}) collective-permute-start(bf16[72,2152]{1,0:T(8,128)(2,1)S(1)} %add_convert_fusion.4), channel_id=1, source_target_pairs={{0,128},{32,160},{64,192},{96,224},{128,0},{160,32},{192,64},{224,... | collective-permute-start | bytes 929672 | tf_op jit(solution)/shard_map/ppermute | solution.py:36
  294.4 6.1 %collective-permute-done.20 = bf16[2152,72]{0,1:T(8,128)(2,1)S(1)} collective-permute-done((bf16[2152,72]{0,1:T(8,128)(2,1)S(1)}, bf16[2152,72]{0,1:T(8,128)(2,1)S(1)}, u32[]{:S(2)}, u32[]{:S(2)}) %collective-permute-start.20) | collective-permute-done | bytes 309920 | tf_op jit(solution)/shard_map/ppermute | solution.py:36
  301.4 2.5 collective-permute-done.16
  (124 shorter events, 29.4 us)
Async XLA Ops:
  7.2 9.1 %copy-start = (bf16[1,192,1152]{2,1,0:T(8,128)(2,1)S(1)}, bf16[1,192,1152]{2,1,0:T(8,128)(2,1)}, u32[]{:S(2)}) copy-start(bf16[1,192,1152]{2,1,0:T(8,128)(2,1)} %param.5) | copy-start | bytes 1327108
  7.2 50.4 %all-gather.3.cloned.1.call-start = ((), (), s32[]{:S(2)}) async-start(), calls=%async_computation.2 | async-start | bytes 2820096 | tf_op jit(solution)/shard_map/all_gather | solution.py:105
  7.9 52.0 %copy-start.12 = (f32[1152]{0:T(1024)S(1)}, f32[1152]{0:T(1024)}, u32[]{:S(2)}) copy-start(f32[1152]{0:T(1024)} %param.6) | copy-start | bytes 13828
  7.9 99.8 %all-gather.5.cloned.1.call-start = ((), (), s32[]{:S(2)}) async-start(), calls=%async_computation.3 | async-start | bytes 2820096 | tf_op jit(solution)/shard_map/all_gather | solution.py:107
  8.7 217.3 %reduce-scatter.9.cloned.1.call-start = ((), (), s32[]{:S(2)}) async-start(), calls=%async_computation.5 | async-start | bytes 2820096
  11.6 1.8 collective-permute-start.3
  13.4 47.5 %copy-start.13 = (f32[192]{0:T(256)}, f32[192]{0:T(256)S(1)}, u32[]{:S(2)}) copy-start(f32[192]{0:T(256)S(1)} %broadcast_multiply_fusion.2) | copy-start | bytes 2308
  13.5 46.2 %copy-start.10 = (bf16[96,1152]{1,0:T(8,128)(2,1)}, bf16[96,1152]{1,0:T(8,128)(2,1)S(1)}, u32[]{:S(2)}) copy-start(bf16[96,1152]{1,0:T(8,128)(2,1)S(1)} %collective-permute-done.3) | copy-start | bytes 663556
  14.3 43.7 %collective-permute-start.4 = (bf16[192,1152]{1,0:T(8,128)(2,1)}, bf16[192,1152]{1,0:T(8,128)(2,1)}, u32[]{:S(2)}, u32[]{:S(2)}) collective-permute-start(bf16[192,1152]{1,0:T(8,128)(2,1)} %pad_maximum_fusion.3), channel_id=1, source_target_pairs={{28,0},{0,4},{4,8},{8,12},{12,16},{16,20},{20,24},{24,28},{29,1},{... | collective-permute-start | bytes 1327112 | tf_op jit(solution)/shard_map/ppermute | solution.py:16
  57.6 70.9 %collective-permute-start = (bf16[576,2152]{1,0:T(8,128)(2,1)}, bf16[576,2152]{1,0:T(8,128)(2,1)}, u32[]{:S(2)}, u32[]{:S(2)}) collective-permute-start(bf16[576,2152]{1,0:T(8,128)(2,1)} %all-gather.3.cloned.1.call-done), channel_id=1, source_target_pairs={{0,2},{2,0},{1,3},{3,1},{4,6},{6,4},{5,7},{7,5},{8,10},{10,8},{9,1... | collective-permute-start | bytes 7437320 | tf_op jit(solution)/shard_map/ppermute | solution.py:20
  57.6 3.4 %copy-start.15 = (f32[192]{0:T(256)}, f32[192]{0:T(256)S(1)}, u32[]{:S(2)}) copy-start(f32[192]{0:T(256)S(1)} %add_rsqrt_fusion) | copy-start | bytes 2308
  57.6 12.9 %collective-permute-start.8 = (bf16[192,1152]{1,0:T(8,128)(2,1)}, bf16[192,1152]{1,0:T(8,128)(2,1)}, u32[]{:S(2)}, u32[]{:S(2)}) collective-permute-start(bf16[192,1152]{1,0:T(8,128)(2,1)} %pad_maximum_fusion.3), channel_id=1, source_target_pairs={{4,0},{8,4},{12,8},{16,12},{20,16},{24,20},{28,24},{0,28},{5,1},{9... | collective-permute-start | bytes 1327112 | tf_op jit(solution)/shard_map/ppermute | solution.py:16
  58.0 14.9 %collective-permute-start.5 = (bf16[192,1152]{1,0:T(8,128)(2,1)}, bf16[192,1152]{1,0:T(8,128)(2,1)}, u32[]{:S(2)}, u32[]{:S(2)}) collective-permute-start(bf16[192,1152]{1,0:T(8,128)(2,1)} %collective-permute-done.4), channel_id=1, source_target_pairs={{28,0},{0,4},{4,8},{8,12},{12,16},{16,20},{20,24},{24,28},{29,1},{... | collective-permute-start | bytes 1327112 | tf_op jit(solution)/shard_map/ppermute | solution.py:16
  61.0 67.4 %copy-start.6 = (bf16[192,8,1,72]{0,3,2,1:T(8,128)(2,1)}, bf16[192,8,1,72]{0,3,2,1:T(8,128)(2,1)S(1)}, u32[]{:S(2)}) copy-start(bf16[192,8,1,72]{0,3,2,1:T(8,128)(2,1)S(1)} %get-tuple-element.14) | copy-start | bytes 663556
  61.0 67.4 %copy-start.1 = (bf16[192,8,1,72]{0,3,2,1:T(8,128)(2,1)}, bf16[192,8,1,72]{0,3,2,1:T(8,128)(2,1)S(1)}, u32[]{:S(2)}) copy-start(bf16[192,8,1,72]{0,3,2,1:T(8,128)(2,1)S(1)} %get-tuple-element.13) | copy-start | bytes 663556
  61.1 66.5 %copy-start.8 = (bf16[576,2152]{1,0:T(8,128)(2,1)S(1)}, bf16[576,2152]{1,0:T(8,128)(2,1)}, u32[]{:S(2)}) copy-start(bf16[576,2152]{1,0:T(8,128)(2,1)} %all-gather.3.cloned.1.call-done) | copy-start | bytes 7437316
  70.5 40.8 %collective-permute-start.9 = (bf16[192,1152]{1,0:T(8,128)(2,1)}, bf16[192,1152]{1,0:T(8,128)(2,1)}, u32[]{:S(2)}, u32[]{:S(2)}) collective-permute-start(bf16[192,1152]{1,0:T(8,128)(2,1)} %collective-permute-done.8), channel_id=1, source_target_pairs={{4,0},{8,4},{12,8},{16,12},{20,16},{24,20},{28,24},{0,28},{5,1},{9... | collective-permute-start | bytes 1327112 | tf_op jit(solution)/shard_map/ppermute | solution.py:16
  72.9 39.2 %collective-permute-start.6 = (bf16[192,1152]{1,0:T(8,128)(2,1)}, bf16[192,1152]{1,0:T(8,128)(2,1)}, u32[]{:S(2)}, u32[]{:S(2)}) collective-permute-start(bf16[192,1152]{1,0:T(8,128)(2,1)} %collective-permute-done.5), channel_id=1, source_target_pairs={{28,0},{0,4},{4,8},{8,12},{12,16},{16,20},{20,24},{24,28},{29,1},{... | collective-permute-start | bytes 1327112 | tf_op jit(solution)/shard_map/ppermute | solution.py:16
  107.7 26.1 %collective-permute-start.1 = (bf16[2152,576]{0,1:T(8,128)(2,1)}, bf16[2152,576]{0,1:T(8,128)(2,1)S(1)}, u32[]{:S(2)}, u32[]{:S(2)}) collective-permute-start(bf16[2152,576]{0,1:T(8,128)(2,1)} %all-gather.5.cloned.1.call-done), channel_id=1, source_target_pairs={{0,2},{2,0},{1,3},{3,1},{4,6},{6,4},{5,7},{7,5},{8,10},{10,8},{9,1... | collective-permute-start | bytes 7437320 | tf_op jit(solution)/shard_map/ppermute | solution.py:20
  111.2 28.8 %collective-permute-start.10 = (bf16[192,1152]{1,0:T(8,128)(2,1)}, bf16[192,1152]{1,0:T(8,128)(2,1)S(1)}, u32[]{:S(2)}, u32[]{:S(2)}) collective-permute-start(bf16[192,1152]{1,0:T(8,128)(2,1)} %collective-permute-done.9), channel_id=1, source_target_pairs={{4,0},{8,4},{12,8},{16,12},{20,16},{24,20},{28,24},{0,28},{5,1},{9... | collective-permute-start | bytes 1327112 | tf_op jit(solution)/shard_map/ppermute | solution.py:16
  112.1 12.8 %collective-permute-start.7 = (bf16[192,1152]{1,0:T(8,128)(2,1)}, bf16[192,1152]{1,0:T(8,128)(2,1)S(1)}, u32[]{:S(2)}, u32[]{:S(2)}) collective-permute-start(bf16[192,1152]{1,0:T(8,128)(2,1)} %collective-permute-done.6), channel_id=1, source_target_pairs={{28,0},{0,4},{4,8},{8,12},{12,16},{16,20},{20,24},{24,28},{29,1},{... | collective-permute-start | bytes 1327112 | tf_op jit(solution)/shard_map/ppermute | solution.py:16
  128.5 4.3 %copy-start.9 = (bf16[2152,576]{0,1:T(8,128)(2,1)S(1)}, bf16[2152,576]{0,1:T(8,128)(2,1)}, u32[]{:S(2)}) copy-start(bf16[2152,576]{0,1:T(8,128)(2,1)} %all-gather.5.cloned.1.call-done) | copy-start | bytes 7437316
  133.9 6.1 %copy-start.18 = (bf16[2152,576]{0,1:T(8,128)(2,1)}, bf16[2152,576]{0,1:T(8,128)(2,1)S(1)}, u32[]{:S(2)}) copy-start(bf16[2152,576]{0,1:T(8,128)(2,1)S(1)} %collective-permute-done.1) | copy-start | bytes 7437316
  135.1 13.3 %collective-permute-start.2 = (bf16[192,1152]{1,0:T(8,128)(2,1)S(1)}, bf16[192,1152]{1,0:T(8,128)(2,1)S(1)}, u32[]{:S(2)}, u32[]{:S(2)}) collective-permute-start(bf16[192,1152]{1,0:T(8,128)(2,1)S(1)} %pad_maximum_fusion.2), channel_id=1, source_target_pairs={{0,1},{1,0},{2,3},{3,2},{4,5},{5,4},{6,7},{7,6},{8,9},{9,8},{10,11... | collective-permute-start | bytes 1327112 | tf_op jit(solution)/shard_map/ppermute | solution.py:25
  149.5 0.9 copy-start.17
  149.5 0.9 copy-start.20
  155.7 15.9 %copy-start.3 = (bf16[192,1152]{1,0:T(8,128)(2,1)}, bf16[192,1152]{1,0:T(8,128)(2,1)S(1)}, u32[]{:S(2)}) copy-start(bf16[192,1152]{1,0:T(8,128)(2,1)S(1)} %fusion.7) | copy-start | bytes 1327108
  155.8 12.5 %collective-permute-start.11 = (bf16[192,1152]{1,0:T(8,128)(2,1)S(1)}, bf16[192,1152]{1,0:T(8,128)(2,1)S(1)}, u32[]{:S(2)}, u32[]{:S(2)}) collective-permute-start(bf16[192,1152]{1,0:T(8,128)(2,1)S(1)} %fusion.7), channel_id=1, source_target_pairs={{0,1},{1,0},{2,3},{3,2},{4,5},{5,4},{6,7},{7,6},{8,9},{9,8},{10,11... | collective-permute-start | bytes 1327112 | tf_op jit(solution)/shard_map/ppermute | solution.py:25
  173.6 4.8 %collective-permute-start.17 = (bf16[2152,576]{0,1:T(8,128)(2,1)S(1)}, bf16[2152,576]{0,1:T(8,128)(2,1)S(1)}, u32[]{:S(2)}, u32[]{:S(2)}) collective-permute-start(bf16[2152,576]{0,1:T(8,128)(2,1)S(1)} %convolution_convert_fusion), channel_id=1, source_target_pairs={{0,2},{2,0},{1,3},{3,1},{4,6},{6,4},{5,7},{7,5},{8,10},{10,8},{9,1... | collective-permute-start | bytes 7437320 | tf_op jit(solution)/shard_map/ppermute | solution.py:20
  180.9 91.7 %reduce-scatter.7.cloned.1.call-start = ((), (), s32[]{:S(2)}) async-start(), calls=%async_computation.4 | async-start | bytes 2820096
  181.2 2.8 copy-start.5
  181.2 3.0 copy-start.19
  184.2 1.8 copy-start.2
  186.0 5.7 %copy-start.7 = (bf16[192,8,1,72]{0,3,2,1:T(8,128)(2,1)S(1)}, bf16[192,8,1,72]{0,3,2,1:T(8,128)(2,1)}, u32[]{:S(2)}) copy-start(bf16[192,8,1,72]{0,3,2,1:T(8,128)(2,1)} %copy-done.6) | copy-start | bytes 663556
  186.8 4.8 %collective-permute-start.13 = (bf16[576,2152]{1,0:T(8,128)(2,1)S(1)}, bf16[576,2152]{1,0:T(8,128)(2,1)S(1)}, u32[]{:S(2)}, u32[]{:S(2)}) collective-permute-start(bf16[576,2152]{1,0:T(8,128)(2,1)S(1)} %convolution_convert_fusion.2), channel_id=1, source_target_pairs={{0,2},{2,0},{1,3},{3,1},{4,6},{6,4},{5,7},{7,5},{8,10},{10,8},{9,1... | collective-permute-start | bytes 7437320 | tf_op jit(solution)/shard_map/ppermute | solution.py:20
  199.8 13.8 %collective-permute-start.12 = (bf16[192,1152]{1,0:T(8,128)(2,1)S(1)}, bf16[192,1152]{1,0:T(8,128)(2,1)S(1)}, u32[]{:S(2)}, u32[]{:S(2)}) collective-permute-start(bf16[192,1152]{1,0:T(8,128)(2,1)S(1)} %pad_maximum_fusion.4), channel_id=1, source_target_pairs={{0,1},{1,0},{2,3},{3,2},{4,5},{5,4},{6,7},{7,6},{8,9},{9,8},{10,11... | collective-permute-start | bytes 1327112 | tf_op jit(solution)/shard_map/ppermute | solution.py:25
  219.4 2.6 copy-start.14
  219.4 2.6 copy-start.16
  219.4 7.9 %copy-start.4 = (bf16[192,1152]{1,0:T(8,128)(2,1)S(1)}, bf16[192,1152]{1,0:T(8,128)(2,1)}, u32[]{:S(2)}) copy-start(bf16[192,1152]{1,0:T(8,128)(2,1)} %copy-done.3) | copy-start | bytes 1327108
  226.0 48.1 %copy-start.11 = (bf16[2152,72]{0,1:T(8,128)(2,1)S(1)}, bf16[2152,72]{0,1:T(8,128)(2,1)}, u32[]{:S(2)}) copy-start(bf16[2152,72]{0,1:T(8,128)(2,1)} %reduce-scatter.9.cloned.1.call-done) | copy-start | bytes 929668
  226.0 48.1 %collective-permute-start.18 = (bf16[2152,72]{0,1:T(8,128)(2,1)}, bf16[2152,72]{0,1:T(8,128)(2,1)S(1)}, u32[]{:S(2)}, u32[]{:S(2)}) collective-permute-start(bf16[2152,72]{0,1:T(8,128)(2,1)} %reduce-scatter.9.cloned.1.call-done), channel_id=1, source_target_pairs={{0,32},{32,0},{64,96},{96,64},{128,160},{160,128},{192,224},{224,1... | collective-permute-start | bytes 929672 | tf_op jit(solution)/shard_map/ppermute | solution.py:36
  272.6 7.1 %collective-permute-start.14 = (bf16[72,2152]{1,0:T(8,128)(2,1)}, bf16[72,2152]{1,0:T(8,128)(2,1)S(1)}, u32[]{:S(2)}, u32[]{:S(2)}) collective-permute-start(bf16[72,2152]{1,0:T(8,128)(2,1)} %reduce-scatter.7.cloned.1.call-done), channel_id=1, source_target_pairs={{0,32},{32,0},{64,96},{96,64},{128,160},{160,128},{192,224},{224,1... | collective-permute-start | bytes 929672 | tf_op jit(solution)/shard_map/ppermute | solution.py:36
  274.2 10.0 %collective-permute-start.19 = (bf16[2152,72]{0,1:T(8,128)(2,1)S(1)}, bf16[2152,72]{0,1:T(8,128)(2,1)S(1)}, u32[]{:S(2)}, u32[]{:S(2)}) collective-permute-start(bf16[2152,72]{0,1:T(8,128)(2,1)S(1)} %add_convert_fusion.3), channel_id=1, source_target_pairs={{0,64},{32,96},{64,0},{96,32},{128,192},{160,224},{192,128},{224,1... | collective-permute-start | bytes 929672 | tf_op jit(solution)/shard_map/ppermute | solution.py:36
  280.8 10.4 %collective-permute-start.15 = (bf16[72,2152]{1,0:T(8,128)(2,1)S(1)}, bf16[72,2152]{1,0:T(8,128)(2,1)S(1)}, u32[]{:S(2)}, u32[]{:S(2)}) collective-permute-start(bf16[72,2152]{1,0:T(8,128)(2,1)S(1)} %add_convert_fusion.5), channel_id=1, source_target_pairs={{0,64},{32,96},{64,0},{96,32},{128,192},{160,224},{192,128},{224,1... | collective-permute-start | bytes 929672 | tf_op jit(solution)/shard_map/ppermute | solution.py:36
  284.3 16.2 %collective-permute-start.20 = (bf16[2152,72]{0,1:T(8,128)(2,1)S(1)}, bf16[2152,72]{0,1:T(8,128)(2,1)S(1)}, u32[]{:S(2)}, u32[]{:S(2)}) collective-permute-start(bf16[2152,72]{0,1:T(8,128)(2,1)S(1)} %add_convert_fusion.2), channel_id=1, source_target_pairs={{0,128},{32,160},{64,192},{96,224},{128,0},{160,32},{192,64},{224,... | collective-permute-start | bytes 929672 | tf_op jit(solution)/shard_map/ppermute | solution.py:36
  291.3 12.6 %collective-permute-start.16 = (bf16[72,2152]{1,0:T(8,128)(2,1)S(1)}, bf16[72,2152]{1,0:T(8,128)(2,1)S(1)}, u32[]{:S(2)}, u32[]{:S(2)}) collective-permute-start(bf16[72,2152]{1,0:T(8,128)(2,1)S(1)} %add_convert_fusion.4), channel_id=1, source_target_pairs={{0,128},{32,160},{64,192},{96,224},{128,0},{160,32},{192,64},{224,... | collective-permute-start | bytes 929672 | tf_op jit(solution)/shard_map/ppermute | solution.py:36
Sparse Core Ops, SparseCore 0:
  9.8 47.7 all-gather.2
  59.4 48.3 all-gather.4
  181.0 44.9 reduce-scatter.8
  228.4 44.1 reduce-scatter.6
